TPU v7x, 256 devices: a whole 4x4x8 slice. The times are simulated.
256 devices in a mesh: tile: 64 (over y, z, core), sec: 4 (over x).
Axes of the slice: x: 4, y: 4, z: 8, core: 2. Of those that a mesh axis runs over, the one named last changes fastest.
Arguments:
- voltage: float32 [8192, 512], P('tile', 'sec'), may hold values from -6 to 6
- conductance: float32 [8192, 512], P('tile', 'sec'), may hold values from 0.2 to 2
- reversal: float32 [8192, 512], P('tile', 'sec'), may hold values from -1 to 1
- drive: bfloat16 [8, 8192, 512], P(None, 'tile', 'sec'), may hold values from -6 to 6
- inv_cable: float32 [128, 128], replicated, may hold values from -1 to 1
- owner_map: int32 [8192], P('tile'), may hold values from 0 to 63, as said below
- peer_counts: int32 [64, 64], P('tile'), may hold values from 0 to 4, as said below
- pattern: int32 [4, 8192, 2], P('sec', 'tile'), may hold values from 0 to 31, all different within a row
- transfer: bfloat16 [4, 8192, 2, 128, 128], P('sec', 'tile'), may hold values from -0.01171875 to 0.01171875
Outputs:
- final_voltage: float32 [8192, 512], P('tile', 'sec')
- probe: float32 [8, 4096], P(None, ('tile', 'sec'))
Inputs may be any that keep to these rules, and one draw needn't show every extreme that they name: `owner_map`: every depth tile owns exactly 128 cells; the cells c with c // 128 = u include at most 4 cells of one owner, and exactly 4 of some owner. peer_counts[d, u] is the number of cells c with c // 128 = u and owner_map[c] = d. `pattern`: the 2 contact tiles of one slot and section differ.
All inputs are finite; a program needn't handle non-finite values.
Results may differ from a plain program's by a relative error of at most 0.0029.
Values may be sent and summed in bfloat16 or wider, within the bound.
A program may use at most 64 MiB of HBM per device.

v0:
```python
import jax
import jax.numpy as jnp
from jax import lax
from jax.sharding import PartitionSpec as P

CONTACTS = 4096


TIME_STEP = 0.25
AXIAL = 2.0


def padded_2(block, sides, width):
    for axis, dim in sides:
        count = lax.axis_size(axis)
        forward = [(i, i + 1) for i in range(count - 1)]
        backward = [(target, source) for source, target in forward]
        low = lax.ppermute(
            lax.slice_in_dim(block, block.shape[dim] - width, None, axis=dim), axis, forward
        )
        high = lax.ppermute(lax.slice_in_dim(block, 0, width, axis=dim), axis, backward)
        block = jnp.concatenate([low, block, high], axis=dim)
    return block


def cable_update(voltage_now, conductance, reversal, drive_now, inv_cable):
    padded = padded_2(voltage_now.astype(jnp.bfloat16), (("sec", 1),), 1).astype(voltage_now.dtype)
    columns = jnp.arange(voltage_now.shape[1], dtype=jnp.int32)
    first_col = (columns == 0).astype(jnp.float32)
    last_col = (columns == voltage_now.shape[1] - 1).astype(jnp.float32)
    boundary = first_col * (padded[:, :-2] - voltage_now) + last_col * (padded[:, 2:] - voltage_now)
    driven = drive_now.astype(jnp.float32)
    right_side = voltage_now * (1.0 - TIME_STEP * conductance) + TIME_STEP * (
        conductance * reversal + driven + AXIAL * boundary
    )
    voltage_next = jnp.einsum("ci,ji->cj", right_side, inv_cable, precision=lax.Precision.HIGHEST)
    current = (conductance * (voltage_next - reversal) - driven).astype(jnp.bfloat16)
    return (voltage_next, current)


def on_device(
    voltage, conductance, reversal, drive, inv_cable, owner_map, peer_counts, pattern, transfer
):
    cell_count = voltage.shape[0]
    seg_width = voltage.shape[1]
    step_count = drive.shape[0]
    tile_count = lax.axis_size("tile")
    section_count = lax.axis_size("sec")
    capacity = 2 * cell_count // tile_count
    owners = jnp.arange(tile_count, dtype=jnp.int32)
    member = (owner_map[:, None] == owners[None, :]).astype(jnp.int32)
    rank_within = jnp.sum(jnp.cumsum(member, axis=0) * member, axis=1) - 1
    placed = owner_map * capacity + rank_within
    source_row = (
        jnp.full((tile_count * capacity,), cell_count, jnp.int32)
        .at[placed]
        .set(jnp.arange(cell_count, dtype=jnp.int32))
    )
    blank_row = jnp.zeros((1, seg_width), jnp.bfloat16)

    def advance_send(voltage_now, drive_now):
        voltage_next, current = cable_update(
            voltage_now, conductance, reversal, drive_now, inv_cable
        )
        outgoing = jnp.take(jnp.concatenate([current, blank_row], axis=0), source_row, axis=0)
        outgoing = outgoing.reshape(tile_count, capacity, seg_width)
        arrived = lax.all_to_all(outgoing, "tile", split_axis=0, concat_axis=0, tiled=True)
        return (voltage_next, arrived)

    final_voltage, arrived = lax.scan(advance_send, voltage, drive)
    received = arrived.reshape(step_count, tile_count * capacity, seg_width)
    counts = peer_counts[0]
    end_rows = jnp.cumsum(counts)
    starts = end_rows - counts
    slot_ids = jnp.arange(cell_count, dtype=jnp.int32)
    source = jnp.sum((end_rows[None, :] <= slot_ids[:, None]).astype(jnp.int32), axis=1)
    offset = jnp.sum(jnp.where(source[:, None] == owners[None, :], starts[None, :], 0), axis=1)
    gather_rows = source * capacity + slot_ids - offset
    ordered = jnp.take(received, gather_rows, axis=1)
    weights = transfer[0]
    layout = pattern[0]
    contact_width = weights.shape[3]
    tile_total = CONTACTS // contact_width
    tile_sums = jnp.einsum("tsi,skic->tskc", ordered, weights, preferred_element_type=jnp.float32)
    select = (layout[:, :, None] == jnp.arange(tile_total, dtype=jnp.int32)[None, None, :]).astype(
        jnp.float32
    )
    partial_sum = jnp.einsum("tskc,skq->tqc", tile_sums, select, precision=lax.Precision.HIGHEST)
    partial_sum = partial_sum.reshape(step_count, tile_total * contact_width)
    summed = lax.psum(partial_sum, ("tile", "sec"))
    share_width = summed.shape[1] // (tile_count * section_count)
    position = lax.axis_index("tile") * section_count + lax.axis_index("sec")
    probe_share = lax.dynamic_slice_in_dim(summed, position * share_width, share_width, 1)
    return (final_voltage, probe_share)


def solution(mesh):
    placed = (
        P("tile", "sec"),
        P("tile", "sec"),
        P("tile", "sec"),
        P(None, "tile", "sec"),
        P(),
        P("tile"),
        P("tile", None),
        P("sec", "tile", None),
        P("sec", "tile", None, None, None),
    )
    return jax.shard_map(
        on_device,
        mesh=mesh,
        in_specs=placed,
        out_specs=(P("tile", "sec"), P(None, ("tile", "sec"))),
        check_vma=False,
    )
```

profile of v0, /device:TPU:1, one launch (start us, length us, event | category | flops | bytes accessed | tf_op | source)
XLA Modules:
  0.0 477.9 jit_solution(9085325909894427495)
XLA Ops:
  12.4 0.9 mul.74
  13.3 1.0 scatter_custom_fusion
  14.3 210.3 %while.13 = (s32[]{:T(128)}, f32[128,128]{1,0:T(8,128)S(1)}, bf16[8,64,4,128]{3,2,1,0:T(4,128)(2,1)S(1)}, f32[128,128]{1,0:T(8,128)}, bf16[8,128,128]{2,1,0:T(8,...) while((s32[]{:T(128)}, f32[128,128]{1,0:T(8,128)S(1)}, ...), condition=%wide.region_4.5_spmd, body=%wide.region_3.4_spmd.sunk | while | flops 25629952 | bytes 1626603 | solution.py:70
  14.4 1.3 collective-permute-start
  15.7 4.6 collective-permute-start.1
  21.4 1.3 fusion.52
  22.7 0.9 gather_fusion
  24.3 13.7 %all-to-all-start = ((bf16[64,4,128]{2,1,0:T(4,128)(2,1)}), bf16[64,4,128]{2,1,0:T(4,128)(2,1)S(1)}, u32[]{:S(2)}, u32[]{:S(2)}) async-start(bf16[64,4,128]{2,1,0:T(4,128)(2,1)} %broadcast_select_fusion.2), calls=%async_computation | async-start | bytes 131072 | tf_op jit(solution)/shard_map/while/body/eval_jaxpr/all_to_all | solution.py:67
  38.0 9.8 %all-to-all-done = bf16[64,4,128]{2,1,0:T(4,128)(2,1)S(1)} async-done(((bf16[64,4,128]{2,1,0:T(4,128)(2,1)}), bf16[64,4,128]{2,1,0:T(4,128)(2,1)S(1)}, u32[]{:S(2)}, u32[]{:S(2)}) %all-to-all-start) | async-done | bytes 65568 | tf_op jit(solution)/shard_map/while/body/eval_jaxpr/all_to_all | solution.py:67
  47.9 1.3 collective-permute-start
  49.2 4.6 collective-permute-start.1
  54.9 1.3 fusion.52
  57.8 5.3 %all-to-all-start = ((bf16[64,4,128]{2,1,0:T(4,128)(2,1)}), bf16[64,4,128]{2,1,0:T(4,128)(2,1)S(1)}, u32[]{:S(2)}, u32[]{:S(2)}) async-start(bf16[64,4,128]{2,1,0:T(4,128)(2,1)} %broadcast_select_fusion.2), calls=%async_computation | async-start | bytes 131072 | tf_op jit(solution)/shard_map/while/body/eval_jaxpr/all_to_all | solution.py:67
  63.1 9.9 %all-to-all-done = bf16[64,4,128]{2,1,0:T(4,128)(2,1)S(1)} async-done(((bf16[64,4,128]{2,1,0:T(4,128)(2,1)}), bf16[64,4,128]{2,1,0:T(4,128)(2,1)S(1)}, u32[]{:S(2)}, u32[]{:S(2)}) %all-to-all-start) | async-done | bytes 65568 | tf_op jit(solution)/shard_map/while/body/eval_jaxpr/all_to_all | solution.py:67
  73.2 1.3 collective-permute-start
  74.5 4.6 collective-permute-start.1
  80.2 1.3 fusion.52
  83.1 5.3 %all-to-all-start = ((bf16[64,4,128]{2,1,0:T(4,128)(2,1)}), bf16[64,4,128]{2,1,0:T(4,128)(2,1)S(1)}, u32[]{:S(2)}, u32[]{:S(2)}) async-start(bf16[64,4,128]{2,1,0:T(4,128)(2,1)} %broadcast_select_fusion.2), calls=%async_computation | async-start | bytes 131072 | tf_op jit(solution)/shard_map/while/body/eval_jaxpr/all_to_all | solution.py:67
  88.4 9.9 %all-to-all-done = bf16[64,4,128]{2,1,0:T(4,128)(2,1)S(1)} async-done(((bf16[64,4,128]{2,1,0:T(4,128)(2,1)}), bf16[64,4,128]{2,1,0:T(4,128)(2,1)S(1)}, u32[]{:S(2)}, u32[]{:S(2)}) %all-to-all-start) | async-done | bytes 65568 | tf_op jit(solution)/shard_map/while/body/eval_jaxpr/all_to_all | solution.py:67
  98.4 1.3 collective-permute-start
  99.7 4.6 collective-permute-start.1
  105.4 1.3 fusion.52
  106.7 0.9 gather_fusion
  108.3 5.3 %all-to-all-start = ((bf16[64,4,128]{2,1,0:T(4,128)(2,1)}), bf16[64,4,128]{2,1,0:T(4,128)(2,1)S(1)}, u32[]{:S(2)}, u32[]{:S(2)}) async-start(bf16[64,4,128]{2,1,0:T(4,128)(2,1)} %broadcast_select_fusion.2), calls=%async_computation | async-start | bytes 131072 | tf_op jit(solution)/shard_map/while/body/eval_jaxpr/all_to_all | solution.py:67
  113.6 9.9 %all-to-all-done = bf16[64,4,128]{2,1,0:T(4,128)(2,1)S(1)} async-done(((bf16[64,4,128]{2,1,0:T(4,128)(2,1)}), bf16[64,4,128]{2,1,0:T(4,128)(2,1)S(1)}, u32[]{:S(2)}, u32[]{:S(2)}) %all-to-all-start) | async-done | bytes 65568 | tf_op jit(solution)/shard_map/while/body/eval_jaxpr/all_to_all | solution.py:67
  123.7 1.3 collective-permute-start
  125.0 4.6 collective-permute-start.1
  130.7 1.3 fusion.52
  133.6 5.3 %all-to-all-start = ((bf16[64,4,128]{2,1,0:T(4,128)(2,1)}), bf16[64,4,128]{2,1,0:T(4,128)(2,1)S(1)}, u32[]{:S(2)}, u32[]{:S(2)}) async-start(bf16[64,4,128]{2,1,0:T(4,128)(2,1)} %broadcast_select_fusion.2), calls=%async_computation | async-start | bytes 131072 | tf_op jit(solution)/shard_map/while/body/eval_jaxpr/all_to_all | solution.py:67
  138.9 9.9 %all-to-all-done = bf16[64,4,128]{2,1,0:T(4,128)(2,1)S(1)} async-done(((bf16[64,4,128]{2,1,0:T(4,128)(2,1)}), bf16[64,4,128]{2,1,0:T(4,128)(2,1)S(1)}, u32[]{:S(2)}, u32[]{:S(2)}) %all-to-all-start) | async-done | bytes 65568 | tf_op jit(solution)/shard_map/while/body/eval_jaxpr/all_to_all | solution.py:67
  148.9 1.3 collective-permute-start
  150.2 4.6 collective-permute-start.1
  155.9 1.3 fusion.52
  158.8 5.3 %all-to-all-start = ((bf16[64,4,128]{2,1,0:T(4,128)(2,1)}), bf16[64,4,128]{2,1,0:T(4,128)(2,1)S(1)}, u32[]{:S(2)}, u32[]{:S(2)}) async-start(bf16[64,4,128]{2,1,0:T(4,128)(2,1)} %broadcast_select_fusion.2), calls=%async_computation | async-start | bytes 131072 | tf_op jit(solution)/shard_map/while/body/eval_jaxpr/all_to_all | solution.py:67
  164.1 9.9 %all-to-all-done = bf16[64,4,128]{2,1,0:T(4,128)(2,1)S(1)} async-done(((bf16[64,4,128]{2,1,0:T(4,128)(2,1)}), bf16[64,4,128]{2,1,0:T(4,128)(2,1)S(1)}, u32[]{:S(2)}, u32[]{:S(2)}) %all-to-all-start) | async-done | bytes 65568 | tf_op jit(solution)/shard_map/while/body/eval_jaxpr/all_to_all | solution.py:67
  174.2 1.3 collective-permute-start
  175.5 4.6 collective-permute-start.1
  181.2 1.3 fusion.52
  184.1 5.3 %all-to-all-start = ((bf16[64,4,128]{2,1,0:T(4,128)(2,1)}), bf16[64,4,128]{2,1,0:T(4,128)(2,1)S(1)}, u32[]{:S(2)}, u32[]{:S(2)}) async-start(bf16[64,4,128]{2,1,0:T(4,128)(2,1)} %broadcast_select_fusion.2), calls=%async_computation | async-start | bytes 131072 | tf_op jit(solution)/shard_map/while/body/eval_jaxpr/all_to_all | solution.py:67
  189.4 9.9 %all-to-all-done = bf16[64,4,128]{2,1,0:T(4,128)(2,1)S(1)} async-done(((bf16[64,4,128]{2,1,0:T(4,128)(2,1)}), bf16[64,4,128]{2,1,0:T(4,128)(2,1)S(1)}, u32[]{:S(2)}, u32[]{:S(2)}) %all-to-all-start) | async-done | bytes 65568 | tf_op jit(solution)/shard_map/while/body/eval_jaxpr/all_to_all | solution.py:67
  199.5 1.3 collective-permute-start
  200.7 4.6 collective-permute-start.1
  206.4 1.3 fusion.52
  209.4 5.3 %all-to-all-start = ((bf16[64,4,128]{2,1,0:T(4,128)(2,1)}), bf16[64,4,128]{2,1,0:T(4,128)(2,1)S(1)}, u32[]{:S(2)}, u32[]{:S(2)}) async-start(bf16[64,4,128]{2,1,0:T(4,128)(2,1)} %broadcast_select_fusion.2), calls=%async_computation | async-start | bytes 131072 | tf_op jit(solution)/shard_map/while/body/eval_jaxpr/all_to_all | solution.py:67
  214.7 9.9 %all-to-all-done = bf16[64,4,128]{2,1,0:T(4,128)(2,1)S(1)} async-done(((bf16[64,4,128]{2,1,0:T(4,128)(2,1)}), bf16[64,4,128]{2,1,0:T(4,128)(2,1)S(1)}, u32[]{:S(2)}, u32[]{:S(2)}) %all-to-all-start) | async-done | bytes 65568 | tf_op jit(solution)/shard_map/while/body/eval_jaxpr/all_to_all | solution.py:67
  225.9 4.6 fusion.28
  232.1 237.6 %all-reduce.3.cloned.1.call-done = f32[8,4096]{1,0:T(8,128)} async-done(((f32[8,4096]{1,0:T(8,128)}), f32[8,4096]{1,0:T(8,128)}) %all-reduce.3.cloned.1.call-update) | async-done | bytes 131088 | tf_op jit(solution)/shard_map/psum | solution.py:90
  469.7 1.3 constant_dynamic-slice_fusion
  (144 shorter events, 28.8 us)
Async XLA Ops:
  7.2 462.5 %all-reduce.3.cloned.1.call-start = ((), (), s32[]{:S(2)}) async-start(), calls=%async_computation.1 | async-start | bytes 262144 | tf_op jit(solution)/shard_map/psum | solution.py:90
  14.4 6.0 %collective-permute-start = (bf16[128,1]{1,0:T(8,128)(2,1)S(1)}, bf16[128,1]{1,0:T(8,128)(2,1)S(1)}, u32[]{:S(2)}, u32[]{:S(2)}) collective-permute-start(bf16[128,1]{1,0:T(8,128)(2,1)S(1)} %get-tuple-element.170), channel_id=1, source_target_pairs={{1,0},{2,1},{3,2},{5,4},{6,5},{7,6},{9,8},{10,9},{11,10},{13,12},{... | collective-permute-start | bytes 776 | tf_op jit(solution)/shard_map/while/body/eval_jaxpr/ppermute | solution.py:21
  15.7 5.6 %collective-permute-start.1 = (bf16[128,1]{1,0:T(8,128)(2,1)S(1)}, bf16[128,1]{1,0:T(8,128)(2,1)S(1)}, u32[]{:S(2)}, u32[]{:S(2)}) collective-permute-start(bf16[128,1]{1,0:T(8,128)(2,1)S(1)} %get-tuple-element.171), channel_id=1, source_target_pairs={{0,1},{1,2},{2,3},{4,5},{5,6},{6,7},{8,9},{9,10},{10,11},{12,13},{... | collective-permute-start | bytes 776 | tf_op jit(solution)/shard_map/while/body/eval_jaxpr/ppermute | solution.py:18
  24.3 23.5 %all-to-all-start = ((bf16[64,4,128]{2,1,0:T(4,128)(2,1)}), bf16[64,4,128]{2,1,0:T(4,128)(2,1)S(1)}, u32[]{:S(2)}, u32[]{:S(2)}) async-start(bf16[64,4,128]{2,1,0:T(4,128)(2,1)} %broadcast_select_fusion.2), calls=%async_computation | async-start | bytes 131072 | tf_op jit(solution)/shard_map/while/body/eval_jaxpr/all_to_all | solution.py:67
  47.9 6.0 %collective-permute-start = (bf16[128,1]{1,0:T(8,128)(2,1)S(1)}, bf16[128,1]{1,0:T(8,128)(2,1)S(1)}, u32[]{:S(2)}, u32[]{:S(2)}) collective-permute-start(bf16[128,1]{1,0:T(8,128)(2,1)S(1)} %get-tuple-element.170), channel_id=1, source_target_pairs={{1,0},{2,1},{3,2},{5,4},{6,5},{7,6},{9,8},{10,9},{11,10},{13,12},{... | collective-permute-start | bytes 776 | tf_op jit(solution)/shard_map/while/body/eval_jaxpr/ppermute | solution.py:21
  49.2 5.6 %collective-permute-start.1 = (bf16[128,1]{1,0:T(8,128)(2,1)S(1)}, bf16[128,1]{1,0:T(8,128)(2,1)S(1)}, u32[]{:S(2)}, u32[]{:S(2)}) collective-permute-start(bf16[128,1]{1,0:T(8,128)(2,1)S(1)} %get-tuple-element.171), channel_id=1, source_target_pairs={{0,1},{1,2},{2,3},{4,5},{5,6},{6,7},{8,9},{9,10},{10,11},{12,13},{... | collective-permute-start | bytes 776 | tf_op jit(solution)/shard_map/while/body/eval_jaxpr/ppermute | solution.py:18
  57.8 15.2 %all-to-all-start = ((bf16[64,4,128]{2,1,0:T(4,128)(2,1)}), bf16[64,4,128]{2,1,0:T(4,128)(2,1)S(1)}, u32[]{:S(2)}, u32[]{:S(2)}) async-start(bf16[64,4,128]{2,1,0:T(4,128)(2,1)} %broadcast_select_fusion.2), calls=%async_computation | async-start | bytes 131072 | tf_op jit(solution)/shard_map/while/body/eval_jaxpr/all_to_all | solution.py:67
  73.2 6.0 %collective-permute-start = (bf16[128,1]{1,0:T(8,128)(2,1)S(1)}, bf16[128,1]{1,0:T(8,128)(2,1)S(1)}, u32[]{:S(2)}, u32[]{:S(2)}) collective-permute-start(bf16[128,1]{1,0:T(8,128)(2,1)S(1)} %get-tuple-element.170), channel_id=1, source_target_pairs={{1,0},{2,1},{3,2},{5,4},{6,5},{7,6},{9,8},{10,9},{11,10},{13,12},{... | collective-permute-start | bytes 776 | tf_op jit(solution)/shard_map/while/body/eval_jaxpr/ppermute | solution.py:21
  74.5 5.6 %collective-permute-start.1 = (bf16[128,1]{1,0:T(8,128)(2,1)S(1)}, bf16[128,1]{1,0:T(8,128)(2,1)S(1)}, u32[]{:S(2)}, u32[]{:S(2)}) collective-permute-start(bf16[128,1]{1,0:T(8,128)(2,1)S(1)} %get-tuple-element.171), channel_id=1, source_target_pairs={{0,1},{1,2},{2,3},{4,5},{5,6},{6,7},{8,9},{9,10},{10,11},{12,13},{... | collective-permute-start | bytes 776 | tf_op jit(solution)/shard_map/while/body/eval_jaxpr/ppermute | solution.py:18
  83.1 15.2 %all-to-all-start = ((bf16[64,4,128]{2,1,0:T(4,128)(2,1)}), bf16[64,4,128]{2,1,0:T(4,128)(2,1)S(1)}, u32[]{:S(2)}, u32[]{:S(2)}) async-start(bf16[64,4,128]{2,1,0:T(4,128)(2,1)} %broadcast_select_fusion.2), calls=%async_computation | async-start | bytes 131072 | tf_op jit(solution)/shard_map/while/body/eval_jaxpr/all_to_all | solution.py:67
  98.4 6.0 %collective-permute-start = (bf16[128,1]{1,0:T(8,128)(2,1)S(1)}, bf16[128,1]{1,0:T(8,128)(2,1)S(1)}, u32[]{:S(2)}, u32[]{:S(2)}) collective-permute-start(bf16[128,1]{1,0:T(8,128)(2,1)S(1)} %get-tuple-element.170), channel_id=1, source_target_pairs={{1,0},{2,1},{3,2},{5,4},{6,5},{7,6},{9,8},{10,9},{11,10},{13,12},{... | collective-permute-start | bytes 776 | tf_op jit(solution)/shard_map/while/body/eval_jaxpr/ppermute | solution.py:21
  99.7 5.6 %collective-permute-start.1 = (bf16[128,1]{1,0:T(8,128)(2,1)S(1)}, bf16[128,1]{1,0:T(8,128)(2,1)S(1)}, u32[]{:S(2)}, u32[]{:S(2)}) collective-permute-start(bf16[128,1]{1,0:T(8,128)(2,1)S(1)} %get-tuple-element.171), channel_id=1, source_target_pairs={{0,1},{1,2},{2,3},{4,5},{5,6},{6,7},{8,9},{9,10},{10,11},{12,13},{... | collective-permute-start | bytes 776 | tf_op jit(solution)/shard_map/while/body/eval_jaxpr/ppermute | solution.py:18
  108.3 15.2 %all-to-all-start = ((bf16[64,4,128]{2,1,0:T(4,128)(2,1)}), bf16[64,4,128]{2,1,0:T(4,128)(2,1)S(1)}, u32[]{:S(2)}, u32[]{:S(2)}) async-start(bf16[64,4,128]{2,1,0:T(4,128)(2,1)} %broadcast_select_fusion.2), calls=%async_computation | async-start | bytes 131072 | tf_op jit(solution)/shard_map/while/body/eval_jaxpr/all_to_all | solution.py:67
  123.7 6.0 %collective-permute-start = (bf16[128,1]{1,0:T(8,128)(2,1)S(1)}, bf16[128,1]{1,0:T(8,128)(2,1)S(1)}, u32[]{:S(2)}, u32[]{:S(2)}) collective-permute-start(bf16[128,1]{1,0:T(8,128)(2,1)S(1)} %get-tuple-element.170), channel_id=1, source_target_pairs={{1,0},{2,1},{3,2},{5,4},{6,5},{7,6},{9,8},{10,9},{11,10},{13,12},{... | collective-permute-start | bytes 776 | tf_op jit(solution)/shard_map/while/body/eval_jaxpr/ppermute | solution.py:21
  125.0 5.6 %collective-permute-start.1 = (bf16[128,1]{1,0:T(8,128)(2,1)S(1)}, bf16[128,1]{1,0:T(8,128)(2,1)S(1)}, u32[]{:S(2)}, u32[]{:S(2)}) collective-permute-start(bf16[128,1]{1,0:T(8,128)(2,1)S(1)} %get-tuple-element.171), channel_id=1, source_target_pairs={{0,1},{1,2},{2,3},{4,5},{5,6},{6,7},{8,9},{9,10},{10,11},{12,13},{... | collective-permute-start | bytes 776 | tf_op jit(solution)/shard_map/while/body/eval_jaxpr/ppermute | solution.py:18
  133.6 15.2 %all-to-all-start = ((bf16[64,4,128]{2,1,0:T(4,128)(2,1)}), bf16[64,4,128]{2,1,0:T(4,128)(2,1)S(1)}, u32[]{:S(2)}, u32[]{:S(2)}) async-start(bf16[64,4,128]{2,1,0:T(4,128)(2,1)} %broadcast_select_fusion.2), calls=%async_computation | async-start | bytes 131072 | tf_op jit(solution)/shard_map/while/body/eval_jaxpr/all_to_all | solution.py:67
  148.9 6.0 %collective-permute-start = (bf16[128,1]{1,0:T(8,128)(2,1)S(1)}, bf16[128,1]{1,0:T(8,128)(2,1)S(1)}, u32[]{:S(2)}, u32[]{:S(2)}) collective-permute-start(bf16[128,1]{1,0:T(8,128)(2,1)S(1)} %get-tuple-element.170), channel_id=1, source_target_pairs={{1,0},{2,1},{3,2},{5,4},{6,5},{7,6},{9,8},{10,9},{11,10},{13,12},{... | collective-permute-start | bytes 776 | tf_op jit(solution)/shard_map/while/body/eval_jaxpr/ppermute | solution.py:21
  150.2 5.6 %collective-permute-start.1 = (bf16[128,1]{1,0:T(8,128)(2,1)S(1)}, bf16[128,1]{1,0:T(8,128)(2,1)S(1)}, u32[]{:S(2)}, u32[]{:S(2)}) collective-permute-start(bf16[128,1]{1,0:T(8,128)(2,1)S(1)} %get-tuple-element.171), channel_id=1, source_target_pairs={{0,1},{1,2},{2,3},{4,5},{5,6},{6,7},{8,9},{9,10},{10,11},{12,13},{... | collective-permute-start | bytes 776 | tf_op jit(solution)/shard_map/while/body/eval_jaxpr/ppermute | solution.py:18
  158.8 15.2 %all-to-all-start = ((bf16[64,4,128]{2,1,0:T(4,128)(2,1)}), bf16[64,4,128]{2,1,0:T(4,128)(2,1)S(1)}, u32[]{:S(2)}, u32[]{:S(2)}) async-start(bf16[64,4,128]{2,1,0:T(4,128)(2,1)} %broadcast_select_fusion.2), calls=%async_computation | async-start | bytes 131072 | tf_op jit(solution)/shard_map/while/body/eval_jaxpr/all_to_all | solution.py:67
  174.2 6.0 %collective-permute-start = (bf16[128,1]{1,0:T(8,128)(2,1)S(1)}, bf16[128,1]{1,0:T(8,128)(2,1)S(1)}, u32[]{:S(2)}, u32[]{:S(2)}) collective-permute-start(bf16[128,1]{1,0:T(8,128)(2,1)S(1)} %get-tuple-element.170), channel_id=1, source_target_pairs={{1,0},{2,1},{3,2},{5,4},{6,5},{7,6},{9,8},{10,9},{11,10},{13,12},{... | collective-permute-start | bytes 776 | tf_op jit(solution)/shard_map/while/body/eval_jaxpr/ppermute | solution.py:21
  175.5 5.6 %collective-permute-start.1 = (bf16[128,1]{1,0:T(8,128)(2,1)S(1)}, bf16[128,1]{1,0:T(8,128)(2,1)S(1)}, u32[]{:S(2)}, u32[]{:S(2)}) collective-permute-start(bf16[128,1]{1,0:T(8,128)(2,1)S(1)} %get-tuple-element.171), channel_id=1, source_target_pairs={{0,1},{1,2},{2,3},{4,5},{5,6},{6,7},{8,9},{9,10},{10,11},{12,13},{... | collective-permute-start | bytes 776 | tf_op jit(solution)/shard_map/while/body/eval_jaxpr/ppermute | solution.py:18
  184.1 15.2 %all-to-all-start = ((bf16[64,4,128]{2,1,0:T(4,128)(2,1)}), bf16[64,4,128]{2,1,0:T(4,128)(2,1)S(1)}, u32[]{:S(2)}, u32[]{:S(2)}) async-start(bf16[64,4,128]{2,1,0:T(4,128)(2,1)} %broadcast_select_fusion.2), calls=%async_computation | async-start | bytes 131072 | tf_op jit(solution)/shard_map/while/body/eval_jaxpr/all_to_all | solution.py:67
  199.5 6.0 %collective-permute-start = (bf16[128,1]{1,0:T(8,128)(2,1)S(1)}, bf16[128,1]{1,0:T(8,128)(2,1)S(1)}, u32[]{:S(2)}, u32[]{:S(2)}) collective-permute-start(bf16[128,1]{1,0:T(8,128)(2,1)S(1)} %get-tuple-element.170), channel_id=1, source_target_pairs={{1,0},{2,1},{3,2},{5,4},{6,5},{7,6},{9,8},{10,9},{11,10},{13,12},{... | collective-permute-start | bytes 776 | tf_op jit(solution)/shard_map/while/body/eval_jaxpr/ppermute | solution.py:21
  200.7 5.6 %collective-permute-start.1 = (bf16[128,1]{1,0:T(8,128)(2,1)S(1)}, bf16[128,1]{1,0:T(8,128)(2,1)S(1)}, u32[]{:S(2)}, u32[]{:S(2)}) collective-permute-start(bf16[128,1]{1,0:T(8,128)(2,1)S(1)} %get-tuple-element.171), channel_id=1, source_target_pairs={{0,1},{1,2},{2,3},{4,5},{5,6},{6,7},{8,9},{9,10},{10,11},{12,13},{... | collective-permute-start | bytes 776 | tf_op jit(solution)/shard_map/while/body/eval_jaxpr/ppermute | solution.py:18
  209.4 15.2 %all-to-all-start = ((bf16[64,4,128]{2,1,0:T(4,128)(2,1)}), bf16[64,4,128]{2,1,0:T(4,128)(2,1)S(1)}, u32[]{:S(2)}, u32[]{:S(2)}) async-start(bf16[64,4,128]{2,1,0:T(4,128)(2,1)} %broadcast_select_fusion.2), calls=%async_computation | async-start | bytes 131072 | tf_op jit(solution)/shard_map/while/body/eval_jaxpr/all_to_all | solution.py:67
  224.6 246.5 %copy-start = (f32[128,128]{1,0:T(8,128)}, f32[128,128]{1,0:T(8,128)S(1)}, u32[]{:S(2)}) copy-start(f32[128,128]{1,0:T(8,128)S(1)} %get-tuple-element.81) | copy-start | bytes 196612
  224.6 6.0 %copy-start.1 = (s32[1,128,2]{1,2,0:T(2,128)S(1)}, s32[1,128,2]{1,2,0:T(2,128)}, u32[]{:S(2)}) copy-start(s32[1,128,2]{1,2,0:T(2,128)} %param.18) | copy-start | bytes 3076
Sparse Core Ops, SparseCore 0:
  232.2 237.4 all-reduce.2
where the time goes:
time: 480 us; the launch traced here: 478 us
  waiting for transfers between devices  323 us (67%)
  starting transfers between devices  97.7 us (20%)
  matrix products  15.6 us (3%)
  local copies, waits for them, and re-layouts  14.6 us (3%)
  between operations  14.1 us (3%)
  other arithmetic  11.6 us (2%)
    psum x1, waiting for transfers between devices, on_device(): summed = lax.psum(partial_sum, ('tile', 'sec'))  238 us
    all_to_all x8, waiting for transfers between devices, advance_send(): lax.all_to_all(outgoing, 'tile', split_axis=0, concat_axis=0, tiled=True)  79.1 us
    all_to_all x8, starting transfers between devices, advance_send(): lax.all_to_all(outgoing, 'tile', split_axis=0, concat_axis=0, tiled=True)  50.8 us
    ppermute x8, starting transfers between devices, padded_2(): lax.ppermute(lax.slice_in_dim(block, block.shape[dim] - width, None, axis...  36.6 us
    ppermute x8, starting transfers between devices, padded_2(): lax.ppermute(lax.slice_in_dim(block, 0, width, axis=dim), axis, backward)  10.3 us
    dot_general x8, matrix products, cable_update(): jnp.einsum('ci,ji->cj', right_side, inv_cable, precision=lax.Precision.HI...  10.2 us
  transfers between devices with their start and end apart: 25, of which 17 were waited for; matrix products, arithmetic and copies ran while one was open for 0% of the time, Pallas kernels for 0%

commit v1 on v0

v1 whole, which is shorter than its diff:
```python
import functools

import jax
import jax.numpy as jnp
from jax import lax
from jax.experimental import pallas as pl
from jax.experimental.pallas import tpu as pltpu
from jax.sharding import PartitionSpec as P

MESH = pl.DeviceIdType.MESH
F32 = jnp.float32
BF16 = jnp.bfloat16

STEPS = 8
HALF = 4
CAP = 4
ROWS = CAP * HALF
LAGS = 8
TIME_STEP = 0.25


def far_first(index, count):
    half = lax.div(index + 1, 2)
    return count // 2 + half * (1 - 2 * lax.rem(index, 2))


def split(x):
    high = x.astype(BF16)
    return high, (x - high.astype(F32)).astype(BF16)


def kernel(
    ny,
    nz,
    nsec,
    v_ref,
    g_ref,
    e_ref,
    d_ref,
    a_ref,
    own_ref,
    cnt_ref,
    pat_ref,
    w_hbm,
    fv_ref,
    probe_ref,
    w_ref,
    zs,
    hl,
    hr,
    ends,
    got,
    hpad,
    pick,
    place,
    cur,
    outs,
    recv,
    ordered,
    tiles,
    part,
    first,
    mine,
    second,
    w_sem,
    send_sem,
    recv_sem,
):
    chips = ny * nz
    ntile = 2 * chips
    cells, seg = v_ref.shape
    tile = lax.axis_index("tile")
    sec = lax.axis_index("sec")
    core = lax.rem(tile, 2)
    chip = lax.div(tile, 2)
    my_y = lax.div(chip, nz)
    my_z = lax.rem(chip, nz)
    line = core * nsec + sec

    def chip_at(dy, dz):
        return lax.rem(my_y + dy, ny) * nz + lax.rem(my_z + dz, nz)

    def tile_peer(o):
        pair = lax.rem(o, 2 * ny)
        dz = far_first(lax.div(o, 2 * ny), nz)
        dy = far_first(lax.div(pair, 2), ny)
        return chip_at(dy, dz) * 2 + lax.rem(core + 1 + lax.rem(pair, 2), 2)

    def chip_peer(o):
        return chip_at(far_first(lax.rem(o, ny), ny), far_first(lax.div(o, ny), nz))

    w_copy = pltpu.make_async_copy(w_hbm.at[0], w_ref, w_sem)
    w_copy.start()

    barrier = pltpu.get_barrier_semaphore()

    def greet(o, carry):
        pl.semaphore_signal(
            barrier, inc=1, device_id=(tile_peer(o), sec), device_id_type=MESH
        )
        return carry

    lax.fori_loop(0, ntile - 1, greet, 0)
    for step in range(1, nsec):
        other = lax.rem(sec + step, nsec)
        pl.semaphore_signal(
            barrier, inc=1, device_id=(tile, other), device_id_type=MESH
        )
        pl.semaphore_signal(
            barrier, inc=1, device_id=(chip * 2 + 1 - core, other), device_id_type=MESH
        )

    a = a_ref[...]
    a_high, a_low = split(a)
    a_both = jnp.concatenate([a_high, a_low], axis=1)

    def times_cable(x):
        high, low = split(x)
        return jnp.dot(
            a_both, jnp.concatenate([high, high], axis=0), preferred_element_type=F32
        ) + jnp.dot(a_high, low, preferred_element_type=F32)

    gt = g_ref[...].T
    row = lax.broadcasted_iota(jnp.int32, (seg, cells), 0)
    at_end = jnp.where((row == 0) | (row == seg - 1), 0.5, 0.0)
    keep = 1.0 - TIME_STEP * gt - at_end
    leak = gt * e_ref[...].T
    zs[0] = v_ref[...].T
    hl[0] = jnp.broadcast_to(a[:, 0:1] * 0.5, (seg, cells))
    hr[0] = jnp.broadcast_to(a[:, seg - 1 : seg] * 0.5, (seg, cells))

    for k in range(STEPS):
        driven = d_ref[k].astype(F32).T
        rhs = keep * zs[k] + TIME_STEP * (leak + driven)
        if k < STEPS - 1:
            after = times_cable(
                jnp.concatenate([rhs, keep * hl[k], keep * hr[k]], axis=1)
            )
            zs[k + 1] = after[:, :cells]
            hl[k + 1] = after[:, cells : 2 * cells]
            hr[k + 1] = after[:, 2 * cells :]
        else:
            zs[k + 1] = times_cable(rhs)

    for k in range(LAGS):
        ends[pl.ds(k, 1), :] = zs[k, pl.ds(0, 1), :]
        ends[pl.ds(8 + k, 1), :] = zs[k, pl.ds(seg - 1, 1), :]
        ends[pl.ds(16 + k, 1), :] = hl[k, pl.ds(0, 1), :]
        ends[pl.ds(24 + k, 1), :] = hl[k, pl.ds(seg - 1, 1), :]
        ends[pl.ds(32 + k, 1), :] = hr[k, pl.ds(0, 1), :]
        ends[pl.ds(40 + k, 1), :] = hr[k, pl.ds(seg - 1, 1), :]

    own = jnp.broadcast_to(own_ref[...].astype(F32), (cells, cells))
    before = lax.broadcasted_iota(jnp.int32, (cells, cells), 0) < (
        lax.broadcasted_iota(jnp.int32, (cells, cells), 1)
    )
    same = jnp.where(before & (own == own.T), 1.0, 0.0)
    rank = jnp.sum(same, axis=0, keepdims=True)
    placed = own_ref[...] * CAP + rank.astype(jnp.int32)
    blocks = 8
    out_rows = ntile * ROWS
    target = jnp.concatenate([placed * HALF + k for k in range(HALF)], axis=1)

    def build_pick(b, carry):
        size = out_rows // blocks
        base = pl.multiple_of(b * size, size)
        rows = base + lax.broadcasted_iota(jnp.int32, (size, HALF * cells), 0)
        pick[pl.ds(base, size), :] = jnp.where(rows == target, 1.0, 0.0).astype(BF16)
        return carry

    lax.fori_loop(0, blocks, build_pick, 0)

    count = jnp.broadcast_to(cnt_ref[...].astype(F32), (8, ntile)).astype(BF16)
    source = lax.broadcasted_iota(jnp.int32, (ntile, out_rows), 0)
    lane = lax.broadcasted_iota(jnp.int32, (ntile, out_rows), 1)
    lane_source = lax.div(lane, ROWS)
    own_count = jnp.where(source == lane_source, 1.0, 0.0).astype(BF16)
    earlier = jnp.where(source < lane_source, 1.0, 0.0).astype(BF16)
    lane_count = jnp.dot(count, own_count, preferred_element_type=F32)[0:1]
    lane_start = jnp.dot(count, earlier, preferred_element_type=F32)[0:1]
    lane_row = lax.broadcasted_iota(jnp.int32, (1, out_rows), 1)
    lane_rank = lax.rem(lax.div(lane_row, HALF), CAP)
    lane_step = lax.rem(lane_row, HALF)
    slot_row = jnp.where(
        lane_rank < lane_count.astype(jnp.int32),
        (lane_start.astype(jnp.int32) + lane_rank) * HALF + lane_step,
        -1,
    )

    def build_place(b, carry):
        size = cells * HALF // blocks
        base = pl.multiple_of(b * size, size)
        rows = base + lax.broadcasted_iota(jnp.int32, (size, out_rows), 0)
        place[pl.ds(base, size), :] = jnp.where(rows == slot_row, 1.0, 0.0).astype(BF16)
        return carry

    lax.fori_loop(0, blocks, build_place, 0)

    contact = lax.broadcasted_iota(jnp.int32, (chips, cells), 0)
    choose = []
    for t in range(2):
        wide = jnp.broadcast_to(pat_ref[:, t : t + 1].astype(F32), (cells, cells)).T
        choose.append(
            jnp.where(wide[:chips].astype(jnp.int32) == contact, 1.0, 0.0).astype(BF16)
        )
    choose = jnp.concatenate(choose + choose, axis=1)

    pl.semaphore_wait(barrier, ntile - 1 + 2 * (nsec - 1))

    for step in range(1, nsec):
        pltpu.make_async_remote_copy(
            src_ref=ends,
            dst_ref=got.at[sec],
            send_sem=send_sem.at[0],
            recv_sem=recv_sem.at[0],
            device_id=(tile, lax.rem(sec + step, nsec)),
            device_id_type=MESH,
        ).start()
    pltpu.make_async_copy(ends, got.at[sec], recv_sem.at[0]).start()
    hpad[:, :, 0:8, :] = jnp.zeros((nsec, 4, 8, cells), F32)
    pltpu.make_async_copy(got, got, recv_sem.at[0]).wait()

    first_of = [got[s, 0:8, :] for s in range(nsec)]
    last_of = [got[s, 8:16, :] for s in range(nsec)]
    for s in range(nsec):
        for q in range(4):
            hpad[s, q, 8:16, :] = got[s, 16 + 8 * q : 24 + 8 * q, :]
    for j in range(STEPS - 1):
        lasts = [jnp.broadcast_to(x[j : j + 1], (8, cells)) for x in last_of]
        firsts = [jnp.broadcast_to(x[j : j + 1], (8, cells)) for x in first_of]
        for s in range(nsec):
            for q, side in ((0, s - 1), (2, s + 1)):
                if 0 <= side < nsec:
                    end = lasts[side] if q == 0 else firsts[side]
                    first_of[s] += hpad[s, q, pl.ds(7 - j, 8), :] * end
                    last_of[s] += hpad[s, q + 1, pl.ds(7 - j, 8), :] * end
    left = jnp.zeros((8, cells), F32)
    right = jnp.zeros((8, cells), F32)
    for s in range(nsec):
        if s > 0:
            left = jnp.where(sec == s, last_of[s - 1], left)
        if s < nsec - 1:
            right = jnp.where(sec == s, first_of[s + 1], right)

    g = g_ref[...]
    e = e_ref[...]
    for k in range(1, STEPS + 1):
        total = zs[k]
        for j in range(k):
            total += hl[k - 1 - j] * left[j : j + 1] + hr[k - 1 - j] * right[j : j + 1]
        now = total.T
        current = (g * (now - e) - d_ref[k - 1].astype(F32)).astype(BF16)
        c, k_in = divmod(k - 1, HALF)
        cur[c, k_in * cells : (k_in + 1) * cells, :] = current
        if k == STEPS:
            fv_ref[...] = now
        if k_in == HALF - 1:
            packed = jnp.dot(pick[...], cur[c], preferred_element_type=F32)
            outs[c] = packed.astype(BF16).reshape(ntile, ROWS, seg)

            def send(o, carry, c=c):
                peer = tile_peer(o)
                pltpu.make_async_remote_copy(
                    src_ref=outs.at[c, peer],
                    dst_ref=recv.at[c, tile],
                    send_sem=send_sem.at[1 + c],
                    recv_sem=recv_sem.at[1 + c],
                    device_id=(peer, sec),
                    device_id_type=MESH,
                ).start()
                return carry

            lax.fori_loop(0, ntile - 1, send, 0)
            pltpu.make_async_copy(
                outs.at[c, tile], recv.at[c, tile], recv_sem.at[1 + c]
            ).start()

    group = ROWS // HALF
    row16 = lax.broadcasted_iota(jnp.int32, (ROWS, seg), 0)
    masks = [
        jnp.where(lax.div(row16, HALF) == n, 1.0, 0.0).astype(BF16)
        for n in range(group)
    ]
    w_copy.wait()
    for c in range(2):
        pltpu.make_async_copy(recv.at[c], recv.at[c], recv_sem.at[1 + c]).wait()
        ordered[...] = (
            jnp.dot(
                place[...],
                recv[c].reshape(out_rows, seg),
                preferred_element_type=F32,
            )
            .astype(BF16)
            .reshape(cells // group, ROWS, seg)
        )

        def read(n, carry, c=c):
            x = ordered[n]
            left_side = jnp.concatenate([x * mask for mask in masks], axis=1)
            for t in range(2):
                right_side = w_ref[pl.ds(n * group, group), t].reshape(group * seg, -1)
                tiles[c, t, pl.ds(pl.multiple_of(n * ROWS, ROWS), ROWS), :] = jnp.dot(
                    left_side, right_side, preferred_element_type=F32
                )
            return carry

        lax.fori_loop(0, cells // group, read, 0, unroll=4)

        for k_in in range(HALF):
            sums = jnp.concatenate(
                [tiles[c, t, pl.ds(k_in, cells, stride=HALF), :] for t in range(2)],
                axis=0,
            )
            high, low = split(sums)
            part[pl.ds(c * HALF + k_in, chips, stride=STEPS), :] = jnp.dot(
                choose,
                jnp.concatenate([high, low], axis=0),
                preferred_element_type=F32,
            )

    def give(o, carry):
        peer = chip_peer(o)
        pltpu.make_async_remote_copy(
            src_ref=part.at[pl.ds(pl.multiple_of(peer * STEPS, STEPS), STEPS)],
            dst_ref=first.at[chip],
            send_sem=send_sem.at[3],
            recv_sem=recv_sem.at[3],
            device_id=(peer * 2 + core, sec),
            device_id_type=MESH,
        ).start()
        return carry

    lax.fori_loop(0, chips - 1, give, 0)
    pltpu.make_async_copy(
        part.at[pl.ds(pl.multiple_of(chip * STEPS, STEPS), STEPS)],
        first.at[chip],
        recv_sem.at[3],
    ).start()
    pltpu.make_async_copy(first, first, recv_sem.at[3]).wait()
    mine[...] = jnp.sum(first[...], axis=0)

    for step in range(nsec):
        for flip in range(2):
            if step or flip:
                other_sec = lax.rem(sec + step, nsec)
                other_core = lax.rem(core + flip, 2)
                pltpu.make_async_remote_copy(
                    src_ref=mine,
                    dst_ref=second.at[line],
                    send_sem=send_sem.at[4],
                    recv_sem=recv_sem.at[4],
                    device_id=(chip * 2 + other_core, other_sec),
                    device_id_type=MESH,
                ).start()
    pltpu.make_async_copy(mine, second.at[line], recv_sem.at[4]).start()
    pltpu.make_async_copy(second, second, recv_sem.at[4]).wait()
    width = probe_ref.shape[1]
    summed = jnp.sum(second[...], axis=0)
    probe_ref[...] = pltpu.roll(summed, lax.rem(seg - line * width, seg), 1)[:, :width]

    pltpu.make_async_copy(got.at[pl.ds(0, nsec - 1)], got.at[pl.ds(0, nsec - 1)], send_sem.at[0]).wait()
    for c in range(2):
        sent = outs.at[c, pl.ds(0, ntile - 1)]
        pltpu.make_async_copy(sent, sent, send_sem.at[1 + c]).wait()
    given = first.at[pl.ds(0, chips - 1)]
    pltpu.make_async_copy(given, given, send_sem.at[3]).wait()
    shared = second.at[pl.ds(0, 2 * nsec - 1)]
    pltpu.make_async_copy(shared, shared, send_sem.at[4]).wait()


def on_device(ny, nz, nsec, width, voltage, conductance, reversal, drive, inv_cable, owner_map, peer_counts, pattern, transfer):
    cells, seg = voltage.shape
    chips = ny * nz
    ntile = 2 * chips
    vmem = pl.BlockSpec(memory_space=pltpu.VMEM)
    rows = ntile * ROWS
    return pl.pallas_call(
        functools.partial(kernel, ny, nz, nsec),
        out_shape=(
            jax.ShapeDtypeStruct((cells, seg), F32),
            jax.ShapeDtypeStruct((STEPS, width), F32),
        ),
        in_specs=[vmem] * 8 + [pl.BlockSpec(memory_space=pl.ANY)],
        out_specs=(vmem, vmem),
        scratch_shapes=[
            pltpu.VMEM(transfer.shape[1:], BF16),
            pltpu.VMEM((STEPS + 1, seg, cells), F32),
            pltpu.VMEM((LAGS, seg, cells), F32),
            pltpu.VMEM((LAGS, seg, cells), F32),
            pltpu.VMEM((48, cells), F32),
            pltpu.VMEM((nsec, 48, cells), F32),
            pltpu.VMEM((nsec, 4, 16, cells), F32),
            pltpu.VMEM((rows, HALF * cells), BF16),
            pltpu.VMEM((cells * HALF, rows), BF16),
            pltpu.VMEM((2, HALF * cells, seg), BF16),
            pltpu.VMEM((2, ntile, ROWS, seg), BF16),
            pltpu.VMEM((2, ntile, ROWS, seg), BF16),
            pltpu.VMEM((cells // 4, ROWS, seg), BF16),
            pltpu.VMEM((2, 2, cells * HALF, seg), F32),
            pltpu.VMEM((chips * STEPS, seg), F32),
            pltpu.VMEM((chips, STEPS, seg), F32),
            pltpu.VMEM((STEPS, seg), F32),
            pltpu.VMEM((2 * nsec, STEPS, seg), F32),
            pltpu.SemaphoreType.DMA,
            pltpu.SemaphoreType.DMA((5,)),
            pltpu.SemaphoreType.DMA((5,)),
        ],
        compiler_params=pltpu.CompilerParams(
            collective_id=0, has_side_effects=True, vmem_limit_bytes=60 * 1024 * 1024
        ),
        name="cable_probe",
    )(
        voltage,
        conductance,
        reversal,
        drive,
        inv_cable,
        owner_map.reshape(1, -1),
        peer_counts,
        pattern[0],
        transfer,
    )


def solution(mesh):
    ntile, nsec = mesh.shape["tile"], mesh.shape["sec"]
    chips = ntile // 2
    nz = 8 if chips % 8 == 0 else 2
    ny = chips // nz
    width = chips * 128 // (ntile * nsec)
    placed = (
        P("tile", "sec"),
        P("tile", "sec"),
        P("tile", "sec"),
        P(None, "tile", "sec"),
        P(),
        P("tile"),
        P("tile", None),
        P("sec", "tile", None),
        P("sec", "tile", None, None, None),
    )
    return jax.shard_map(
        functools.partial(on_device, ny, nz, nsec, width),
        mesh=mesh,
        in_specs=placed,
        out_specs=(P("tile", "sec"), P(None, ("tile", "sec"))),
        check_vma=False,
    )
```

time: 480 us -> 49.9 us (0.10)
  waiting for transfers between devices: 323 us -> 0 us
  starting transfers between devices: 97.7 us -> 0 us
  Pallas kernels: 0 us -> 44.9 us
  matrix products: 15.6 us -> 0 us
  between operations: 14.1 us -> 0.64 us
  other arithmetic: 11.6 us -> 0 us
  local copies, waits for them, and re-layouts: 14.6 us -> 4.16 us
    psum x1 -> x0, waiting for transfers between devices: 238 us -> none  [on_device(): summed = lax.psum(partial_sum, ('tile', 'sec'))]
    all_to_all x8 -> x0, waiting for transfers between devices: 79.1 us -> none  [advance_send(): lax.all_to_all(outgoing, 'tile', split_axis=0, concat_axis=0, tiled=True)]
    all_to_all x8 -> x0, starting transfers between devices: 50.8 us -> none  [advance_send(): lax.all_to_all(outgoing, 'tile', split_axis=0, concat_axis=0, tiled=True)]
    ppermute x16 -> x0, starting transfers between devices: 46.8 us -> none  [the longest x8 36.6 us: padded_2(): lax.ppermute(lax.slice_in_dim(block, block.shape[dim] - width, None, axis...]
    pallas_call x0 -> x1, Pallas kernels: none -> 44.9 us  [on_device(): pl.pallas_call(functools.partial(kernel, ny, nz, nsec), out_shape=(jax.Sh...]
    dot_general x10 -> x0, matrix products: 15.6 us -> none  [the longest x8 10.2 us: cable_update(): jnp.einsum('ci,ji->cj', right_side, inv_cable, precision=lax.Precision.HI...]
    gather x9 -> x0, local copies, waits for them, and re-layouts: 7.53 us -> none  [the longest x8 6.84 us: advance_send(): jnp.take(jnp.concatenate([current, blank_row], axis=0), source_row, axis=0)]
    select_n x18 -> x0, other arithmetic: 6.87 us -> none  [the longest x16 6.19 us: advance_send(): jnp.take(jnp.concatenate([current, blank_row], axis=0), source_row, axis=0)]
  transfers between devices with their start and end apart: 25 -> 0, of which waited for: 17 -> 0; matrix products, arithmetic and copies ran while one was open for 0% -> 0% of each run, Pallas kernels for 0% -> 0%
where the time goes in v1:
time: 49.9 us; the launch traced here: 49.7 us
  Pallas kernels  44.9 us (90%)
  local copies, waits for them, and re-layouts  4.16 us (8%)
  between operations  0.64 us (1%)
    pallas_call x1, Pallas kernels, on_device(): pl.pallas_call(functools.partial(kernel, ny, nz, nsec), out_shape=(jax.Sh...  44.9 us
    unnamed x3, local copies, waits for them, and re-layouts  4.16 us

profile of v1, /device:TPU:1, one launch (start us, length us, event | category | flops | bytes accessed | tf_op | source)
XLA Modules:
  0.0 49.7 jit_solution(5481604154595676882)
XLA Ops:
  0.6 1.4 %copy.11 = s32[1,128,2]{2,1,0:T(8,128)} copy(s32[1,128,2]{1,2,0:T(2,128)} %param.16) | data formatting | bytes 2048 | tf_op args[7]
  2.0 44.9 %cable_probe.1 = (f32[128,128]{1,0:T(8,128)}, f32[8,16]{1,0:T(8,128)}) custom-call(f32[128,128]{1,0:T(8,128)} %v_ref.1, f32[128,128]{1,0:T(8,128)} %g_ref.1, f32[128,128]{1,0:T(8,128)} %e_ref.1, bf16[8,128,128]{2,1,0:T(8,128)(2,1)} %d_ref.1, f32[128,128]{1,0:T(8,128)} %a_ref.1, s32[1,128]{1,0:T(1,128)} %bitcast.3, s32[1,64]{1,0:T(1,128)} %cnt_ref.1, ...), custom_call_target="tpu_custom_call" | custom-call | tf_op jit(solution)/shard_map/cable_probe/pallas_call | solution.py:377
  46.9 1.5 %copy.14 = f32[128,128]{1,0:T(8,128)} copy(f32[128,128]{1,0:T(8,128)} %get-tuple-element.4) | data formatting | bytes 131072
  48.4 1.3 %copy.15 = f32[8,16]{1,0:T(8,128)} copy(f32[8,16]{1,0:T(8,128)} %get-tuple-element.5) | data formatting | bytes 1024

commit v2 on v1

--- a/solution.py
+++ b/solution.py
@@ -33,6 +33,17 @@
     ny,
     nz,
     nsec,
+    v_hbm,
+    g_hbm,
+    e_hbm,
+    d_hbm,
+    a_hbm,
+    own_hbm,
+    cnt_hbm,
+    pat_hbm,
+    w_hbm,
+    fv_ref,
+    probe_ref,
     v_ref,
     g_ref,
     e_ref,
@@ -41,9 +52,6 @@
     own_ref,
     cnt_ref,
     pat_ref,
-    w_hbm,
-    fv_ref,
-    probe_ref,
     w_ref,
     zs,
     hl,
@@ -51,6 +59,7 @@
     ends,
     got,
     hpad,
+    zpad,
     pick,
     place,
     cur,
@@ -62,7 +71,9 @@
     first,
     mine,
     second,
+    in_sem,
     w_sem,
+    round_sem,
     send_sem,
     recv_sem,
 ):
@@ -89,26 +100,40 @@
     def chip_peer(o):
         return chip_at(far_first(lax.rem(o, ny), ny), far_first(lax.div(o, ny), nz))
 
+    barrier = pltpu.get_barrier_semaphore()
+
+    def signal(sem, peer, peer_sec):
+        pl.semaphore_signal(
+            sem, inc=1, device_id=(peer, peer_sec), device_id_type=MESH
+        )
+
+    for step in range(1, nsec):
+        signal(barrier, tile, lax.rem(sec + step, nsec))
+    for dz in (2, nz - 2, 1, nz - 1):
+        signal(barrier, chip_at(0, dz) * 2 + core, sec)
+    for dy in (2, 1, 3):
+        signal(barrier, chip_at(dy, 0) * 2 + core, sec)
+    signal(barrier, chip * 2 + 1 - core, sec)
+
+    loads = []
+    for n, (src, dst) in enumerate(
+        (
+            (a_hbm, a_ref),
+            (g_hbm, g_ref),
+            (e_hbm, e_ref),
+            (v_hbm, v_ref),
+            (d_hbm, d_ref),
+            (own_hbm, own_ref),
+            (cnt_hbm, cnt_ref),
+            (pat_hbm, pat_ref),
+        )
+    ):
+        loads.append(pltpu.make_async_copy(src, dst, in_sem.at[n]))
+        loads[-1].start()
     w_copy = pltpu.make_async_copy(w_hbm.at[0], w_ref, w_sem)
     w_copy.start()
-
-    barrier = pltpu.get_barrier_semaphore()
-
-    def greet(o, carry):
-        pl.semaphore_signal(
-            barrier, inc=1, device_id=(tile_peer(o), sec), device_id_type=MESH
-        )
-        return carry
-
-    lax.fori_loop(0, ntile - 1, greet, 0)
-    for step in range(1, nsec):
-        other = lax.rem(sec + step, nsec)
-        pl.semaphore_signal(
-            barrier, inc=1, device_id=(tile, other), device_id_type=MESH
-        )
-        pl.semaphore_signal(
-            barrier, inc=1, device_id=(chip * 2 + 1 - core, other), device_id_type=MESH
-        )
+    for load in loads:
+        load.wait()
 
     a = a_ref[...]
     a_high, a_low = split(a)
@@ -129,7 +154,7 @@
     hl[0] = jnp.broadcast_to(a[:, 0:1] * 0.5, (seg, cells))
     hr[0] = jnp.broadcast_to(a[:, seg - 1 : seg] * 0.5, (seg, cells))
 
-    for k in range(STEPS):
+    def advance(k):
         driven = d_ref[k].astype(F32).T
         rhs = keep * zs[k] + TIME_STEP * (leak + driven)
         if k < STEPS - 1:
@@ -142,13 +167,36 @@
         else:
             zs[k + 1] = times_cable(rhs)
 
-    for k in range(LAGS):
-        ends[pl.ds(k, 1), :] = zs[k, pl.ds(0, 1), :]
-        ends[pl.ds(8 + k, 1), :] = zs[k, pl.ds(seg - 1, 1), :]
-        ends[pl.ds(16 + k, 1), :] = hl[k, pl.ds(0, 1), :]
-        ends[pl.ds(24 + k, 1), :] = hl[k, pl.ds(seg - 1, 1), :]
-        ends[pl.ds(32 + k, 1), :] = hr[k, pl.ds(0, 1), :]
-        ends[pl.ds(40 + k, 1), :] = hr[k, pl.ds(seg - 1, 1), :]
+    def offer(c):
+        for k in range(HALF):
+            at = c * HALF + k
+            for n, source in enumerate((zs, hl, hr)):
+                ends[c, pl.ds(2 * HALF * n + k, 1), :] = source[at, pl.ds(0, 1), :]
+                ends[c, pl.ds(2 * HALF * n + HALF + k, 1), :] = source[
+                    at, pl.ds(seg - 1, 1), :
+                ]
+        for step in range(1, nsec):
+            pltpu.make_async_remote_copy(
+                src_ref=ends.at[c],
+                dst_ref=got.at[c, sec],
+                send_sem=send_sem.at[5 + c],
+                recv_sem=recv_sem.at[5 + c],
+                device_id=(tile, lax.rem(sec + step, nsec)),
+                device_id_type=MESH,
+            ).start()
+        pltpu.make_async_copy(ends.at[c], got.at[c, sec], recv_sem.at[5 + c]).start()
+
+    for k in range(HALF - 1):
+        advance(k)
+    pl.semaphore_wait(barrier, nsec - 1 + 8)
+    offer(0)
+    for dz in (2, nz - 2):
+        signal(round_sem.at[0], chip_at(0, dz) * 2 + core, sec)
+    for k in range(HALF - 1, STEPS - 1):
+        advance(k)
+    offer(1)
+    advance(STEPS - 1)
+    hpad[:, :, 0:8, :] = jnp.zeros((nsec, 4, 8, cells), F32)
 
     own = jnp.broadcast_to(own_ref[...].astype(F32), (cells, cells))
     before = lax.broadcasted_iota(jnp.int32, (cells, cells), 0) < (
@@ -169,6 +217,83 @@
         return carry
 
     lax.fori_loop(0, blocks, build_pick, 0)
+
+    def meet(c):
+        pltpu.make_async_copy(got.at[c], got.at[c], recv_sem.at[5 + c]).wait()
+        known = (c + 1) * HALF
+        for s in range(nsec):
+            for q in range(2):
+                zpad[s, q, c * HALF : known, :] = got[c, s, q * HALF : (q + 1) * HALF, :]
+            for q in range(4):
+                hpad[s, q, 8 + c * HALF : 8 + known, :] = got[
+                    c, s, (2 + q) * HALF : (3 + q) * HALF, :
+                ]
+        first_of = [zpad[s, 0, 0:known, :] for s in range(nsec)]
+        last_of = [zpad[s, 1, 0:known, :] for s in range(nsec)]
+        for j in range(known - 1):
+            lasts = [jnp.broadcast_to(x[j : j + 1], (known, cells)) for x in last_of]
+            firsts = [jnp.broadcast_to(x[j : j + 1], (known, cells)) for x in first_of]
+            for s in range(nsec):
+                for q, side in ((0, s - 1), (2, s + 1)):
+                    if 0 <= side < nsec:
+                        end = lasts[side] if q == 0 else firsts[side]
+                        first_of[s] += hpad[s, q, pl.ds(7 - j, known), :] * end
+                        last_of[s] += hpad[s, q + 1, pl.ds(7 - j, known), :] * end
+        left = jnp.zeros((known, cells), F32)
+        right = jnp.zeros((known, cells), F32)
+        for s in range(nsec):
+            if s > 0:
+                left = jnp.where(sec == s, last_of[s - 1], left)
+            if s < nsec - 1:
+                right = jnp.where(sec == s, first_of[s + 1], right)
+        return left, right
+
+    def currents(c):
+        left, right = meet(c)
+        for k_in in range(HALF):
+            k = c * HALF + k_in + 1
+            total = zs[k]
+            for j in range(k):
+                total += (
+                    hl[k - 1 - j] * left[j : j + 1] + hr[k - 1 - j] * right[j : j + 1]
+                )
+            now = total.T
+            driven = d_ref[k - 1].astype(F32)
+            current = (g_ref[...] * (now - e_ref[...]) - driven).astype(BF16)
+            cur[c, k_in * cells : (k_in + 1) * cells, :] = current
+            if k == STEPS:
+                fv_ref[...] = now
+        packed = jnp.dot(pick[...], cur[c], preferred_element_type=F32)
+        outs[c] = packed.astype(BF16).reshape(ntile, ROWS, seg)
+
+    def deliver(c):
+        def send(o, carry):
+            peer = tile_peer(o)
+            pltpu.make_async_remote_copy(
+                src_ref=outs.at[c, peer],
+                dst_ref=recv.at[c, tile],
+                send_sem=send_sem.at[1 + c],
+                recv_sem=recv_sem.at[1 + c],
+                device_id=(peer, sec),
+                device_id_type=MESH,
+            ).start()
+            return carry
+
+        lax.fori_loop(0, ntile - 1, send, 0)
+        pltpu.make_async_copy(
+            outs.at[c, tile], recv.at[c, tile], recv_sem.at[1 + c]
+        ).start()
+
+    pl.semaphore_wait(round_sem.at[0], 2)
+    for dy in (2, 1, 3):
+        signal(round_sem.at[1], chip_at(dy, 0) * 2 + core, sec)
+    currents(0)
+    pl.semaphore_wait(round_sem.at[1], 3)
+    signal(round_sem.at[2], chip * 2 + 1 - core, sec)
+    pl.semaphore_wait(round_sem.at[2], 1)
+    deliver(0)
+    currents(1)
+    deliver(1)
 
     count = jnp.broadcast_to(cnt_ref[...].astype(F32), (8, ntile)).astype(BF16)
     source = lax.broadcasted_iota(jnp.int32, (ntile, out_rows), 0)
@@ -197,83 +322,13 @@
     lax.fori_loop(0, blocks, build_place, 0)
 
     contact = lax.broadcasted_iota(jnp.int32, (chips, cells), 0)
-    choose = []
-    for t in range(2):
-        wide = jnp.broadcast_to(pat_ref[:, t : t + 1].astype(F32), (cells, cells)).T
-        choose.append(
-            jnp.where(wide[:chips].astype(jnp.int32) == contact, 1.0, 0.0).astype(BF16)
-        )
-    choose = jnp.concatenate(choose + choose, axis=1)
-
-    pl.semaphore_wait(barrier, ntile - 1 + 2 * (nsec - 1))
-
-    for step in range(1, nsec):
-        pltpu.make_async_remote_copy(
-            src_ref=ends,
-            dst_ref=got.at[sec],
-            send_sem=send_sem.at[0],
-            recv_sem=recv_sem.at[0],
-            device_id=(tile, lax.rem(sec + step, nsec)),
-            device_id_type=MESH,
-        ).start()
-    pltpu.make_async_copy(ends, got.at[sec], recv_sem.at[0]).start()
-    hpad[:, :, 0:8, :] = jnp.zeros((nsec, 4, 8, cells), F32)
-    pltpu.make_async_copy(got, got, recv_sem.at[0]).wait()
-
-    first_of = [got[s, 0:8, :] for s in range(nsec)]
-    last_of = [got[s, 8:16, :] for s in range(nsec)]
-    for s in range(nsec):
-        for q in range(4):
-            hpad[s, q, 8:16, :] = got[s, 16 + 8 * q : 24 + 8 * q, :]
-    for j in range(STEPS - 1):
-        lasts = [jnp.broadcast_to(x[j : j + 1], (8, cells)) for x in last_of]
-        firsts = [jnp.broadcast_to(x[j : j + 1], (8, cells)) for x in first_of]
-        for s in range(nsec):
-            for q, side in ((0, s - 1), (2, s + 1)):
-                if 0 <= side < nsec:
-                    end = lasts[side] if q == 0 else firsts[side]
-                    first_of[s] += hpad[s, q, pl.ds(7 - j, 8), :] * end
-                    last_of[s] += hpad[s, q + 1, pl.ds(7 - j, 8), :] * end
-    left = jnp.zeros((8, cells), F32)
-    right = jnp.zeros((8, cells), F32)
-    for s in range(nsec):
-        if s > 0:
-            left = jnp.where(sec == s, last_of[s - 1], left)
-        if s < nsec - 1:
-            right = jnp.where(sec == s, first_of[s + 1], right)
-
-    g = g_ref[...]
-    e = e_ref[...]
-    for k in range(1, STEPS + 1):
-        total = zs[k]
-        for j in range(k):
-            total += hl[k - 1 - j] * left[j : j + 1] + hr[k - 1 - j] * right[j : j + 1]
-        now = total.T
-        current = (g * (now - e) - d_ref[k - 1].astype(F32)).astype(BF16)
-        c, k_in = divmod(k - 1, HALF)
-        cur[c, k_in * cells : (k_in + 1) * cells, :] = current
-        if k == STEPS:
-            fv_ref[...] = now
-        if k_in == HALF - 1:
-            packed = jnp.dot(pick[...], cur[c], preferred_element_type=F32)
-            outs[c] = packed.astype(BF16).reshape(ntile, ROWS, seg)
-
-            def send(o, carry, c=c):
-                peer = tile_peer(o)
-                pltpu.make_async_remote_copy(
-                    src_ref=outs.at[c, peer],
-                    dst_ref=recv.at[c, tile],
-                    send_sem=send_sem.at[1 + c],
-                    recv_sem=recv_sem.at[1 + c],
-                    device_id=(peer, sec),
-                    device_id_type=MESH,
-                ).start()
-                return carry
-
-            lax.fori_loop(0, ntile - 1, send, 0)
-            pltpu.make_async_copy(
-                outs.at[c, tile], recv.at[c, tile], recv_sem.at[1 + c]
-            ).start()
+    choose = jnp.concatenate(
+        [
+            jnp.where(pat_ref[t : t + 1, :] == contact, 1.0, 0.0).astype(BF16)
+            for t in (0, 1, 0, 1)
+        ],
+        axis=1,
+    )
 
     group = ROWS // HALF
     row16 = lax.broadcasted_iota(jnp.int32, (ROWS, seg), 0)
@@ -358,8 +413,9 @@
     summed = jnp.sum(second[...], axis=0)
     probe_ref[...] = pltpu.roll(summed, lax.rem(seg - line * width, seg), 1)[:, :width]
 
-    pltpu.make_async_copy(got.at[pl.ds(0, nsec - 1)], got.at[pl.ds(0, nsec - 1)], send_sem.at[0]).wait()
     for c in range(2):
+        told = got.at[c, pl.ds(0, nsec - 1)]
+        pltpu.make_async_copy(told, told, send_sem.at[5 + c]).wait()
         sent = outs.at[c, pl.ds(0, ntile - 1)]
         pltpu.make_async_copy(sent, sent, send_sem.at[1 + c]).wait()
     given = first.at[pl.ds(0, chips - 1)]
@@ -380,16 +436,25 @@
             jax.ShapeDtypeStruct((cells, seg), F32),
             jax.ShapeDtypeStruct((STEPS, width), F32),
         ),
-        in_specs=[vmem] * 8 + [pl.BlockSpec(memory_space=pl.ANY)],
+        in_specs=[pl.BlockSpec(memory_space=pl.ANY)] * 9,
         out_specs=(vmem, vmem),
         scratch_shapes=[
+            pltpu.VMEM((cells, seg), F32),
+            pltpu.VMEM((cells, seg), F32),
+            pltpu.VMEM((cells, seg), F32),
+            pltpu.VMEM((STEPS, cells, seg), BF16),
+            pltpu.VMEM((seg, seg), F32),
+            pltpu.VMEM((1, cells), jnp.int32),
+            pltpu.VMEM((1, ntile), jnp.int32),
+            pltpu.VMEM((2, cells), jnp.int32),
             pltpu.VMEM(transfer.shape[1:], BF16),
             pltpu.VMEM((STEPS + 1, seg, cells), F32),
             pltpu.VMEM((LAGS, seg, cells), F32),
             pltpu.VMEM((LAGS, seg, cells), F32),
-            pltpu.VMEM((48, cells), F32),
-            pltpu.VMEM((nsec, 48, cells), F32),
+            pltpu.VMEM((2, 6 * HALF, cells), F32),
+            pltpu.VMEM((2, nsec, 6 * HALF, cells), F32),
             pltpu.VMEM((nsec, 4, 16, cells), F32),
+            pltpu.VMEM((nsec, 2, 8, cells), F32),
             pltpu.VMEM((rows, HALF * cells), BF16),
             pltpu.VMEM((cells * HALF, rows), BF16),
             pltpu.VMEM((2, HALF * cells, seg), BF16),
@@ -401,9 +466,11 @@
             pltpu.VMEM((chips, STEPS, seg), F32),
             pltpu.VMEM((STEPS, seg), F32),
             pltpu.VMEM((2 * nsec, STEPS, seg), F32),
+            pltpu.SemaphoreType.DMA((8,)),
             pltpu.SemaphoreType.DMA,
-            pltpu.SemaphoreType.DMA((5,)),
-            pltpu.SemaphoreType.DMA((5,)),
+            pltpu.SemaphoreType.REGULAR((3,)),
+            pltpu.SemaphoreType.DMA((7,)),
+            pltpu.SemaphoreType.DMA((7,)),
         ],
         compiler_params=pltpu.CompilerParams(
             collective_id=0, has_side_effects=True, vmem_limit_bytes=60 * 1024 * 1024
@@ -417,7 +484,7 @@
         inv_cable,
         owner_map.reshape(1, -1),
         peer_counts,
-        pattern[0],
+        pattern[0].T,
         transfer,
     )
 

time: 49.9 us -> 46.3 us (0.928)
  Pallas kernels: 44.9 us -> 42.7 us
  local copies, waits for them, and re-layouts: 4.16 us -> 2.74 us
    pallas_call x1, Pallas kernels: 44.9 us -> 42.7 us  [on_device(): pl.pallas_call(functools.partial(kernel, ny, nz, nsec), out_shape=(jax.Sh...]
    unnamed x3 -> x2, local copies, waits for them, and re-layouts: 4.16 us -> 2.74 us
where the time goes in v2:
time: 46.3 us; the launch traced here: 46.1 us
  Pallas kernels  42.7 us (92%)
  local copies, waits for them, and re-layouts  2.74 us (6%)
  between operations  0.64 us (1%)
    pallas_call x1, Pallas kernels, on_device(): pl.pallas_call(functools.partial(kernel, ny, nz, nsec), out_shape=(jax.Sh...  42.7 us
    unnamed x2, local copies, waits for them, and re-layouts  2.74 us

profile of v2, /device:TPU:1, one launch (start us, length us, event | category | flops | bytes accessed | tf_op | source)
XLA Modules:
  0.0 46.1 jit_solution(9578187426696336741)
XLA Ops:
  0.6 42.7 %cable_probe.1 = (f32[128,128]{1,0:T(8,128)}, f32[8,16]{1,0:T(8,128)}) custom-call(f32[128,128]{1,0:T(8,128)} %v_hbm.1, f32[128,128]{1,0:T(8,128)} %g_hbm.1, f32[128,128]{1,0:T(8,128)} %e_hbm.1, bf16[8,128,128]{2,1,0:T(8,128)(2,1)} %d_hbm.1, f32[128,128]{1,0:T(8,128)} %a_hbm.1, s32[1,128]{1,0:T(1,128)} %bitcast.5, s32[1,64]{1,0:T(1,128)} %cnt_hbm.1, ...), custom_call_target="tpu_custom_call" | custom-call | tf_op jit(solution)/shard_map/cable_probe/pallas_call | solution.py:433
  43.4 1.5 %copy.13 = f32[128,128]{1,0:T(8,128)} copy(f32[128,128]{1,0:T(8,128)} %get-tuple-element.4) | data formatting | bytes 131072
  44.8 1.3 %copy.14 = f32[8,16]{1,0:T(8,128)} copy(f32[8,16]{1,0:T(8,128)} %get-tuple-element.5) | data formatting | bytes 1024

commit v3 on v2

--- a/solution.py
+++ b/solution.py
@@ -68,6 +68,7 @@
     ordered,
     tiles,
     part,
+    partial,
     first,
     mine,
     second,
@@ -88,17 +89,18 @@
     my_z = lax.rem(chip, nz)
     line = core * nsec + sec
 
-    def chip_at(dy, dz):
-        return lax.rem(my_y + dy, ny) * nz + lax.rem(my_z + dz, nz)
-
-    def tile_peer(o):
-        pair = lax.rem(o, 2 * ny)
-        dz = far_first(lax.div(o, 2 * ny), nz)
-        dy = far_first(lax.div(pair, 2), ny)
-        return chip_at(dy, dz) * 2 + lax.rem(core + 1 + lax.rem(pair, 2), 2)
-
-    def chip_peer(o):
-        return chip_at(far_first(lax.rem(o, ny), ny), far_first(lax.div(o, ny), nz))
+    base_y = [lax.rem(my_y + dy, ny) * nz for dy in range(ny)]
+    at_z = [lax.rem(my_z + dz, nz) for dz in range(nz)]
+    y_order = (2, 1, 3)
+    far = (4, 3, 5)
+    near = (2, 6, 1, 7)
+
+    def along_y(body):
+        def step(index, carry):
+            body(lax.rem(my_y + far_first(index, ny), ny) * nz)
+            return carry
+
+        lax.fori_loop(0, ny - 1, step, 0)
 
     barrier = pltpu.get_barrier_semaphore()
 
@@ -106,14 +108,6 @@
         pl.semaphore_signal(
             sem, inc=1, device_id=(peer, peer_sec), device_id_type=MESH
         )
-
-    for step in range(1, nsec):
-        signal(barrier, tile, lax.rem(sec + step, nsec))
-    for dz in (2, nz - 2, 1, nz - 1):
-        signal(barrier, chip_at(0, dz) * 2 + core, sec)
-    for dy in (2, 1, 3):
-        signal(barrier, chip_at(dy, 0) * 2 + core, sec)
-    signal(barrier, chip * 2 + 1 - core, sec)
 
     loads = []
     for n, (src, dst) in enumerate(
@@ -130,10 +124,19 @@
     ):
         loads.append(pltpu.make_async_copy(src, dst, in_sem.at[n]))
         loads[-1].start()
+    for step in range(1, nsec):
+        signal(barrier, tile, lax.rem(sec + step, nsec))
+    for dz in (2, nz - 2, 1, nz - 1):
+        signal(barrier, (base_y[0] + at_z[dz]) * 2 + core, sec)
+    for dy in (2, 1, 3, 0):
+        if dy:
+            signal(barrier, (base_y[dy] + my_z) * 2 + core, sec)
+        signal(barrier, (base_y[dy] + my_z) * 2 + 1 - core, sec)
+
+    for load in loads[:5]:
+        load.wait()
     w_copy = pltpu.make_async_copy(w_hbm.at[0], w_ref, w_sem)
     w_copy.start()
-    for load in loads:
-        load.wait()
 
     a = a_ref[...]
     a_high, a_low = split(a)
@@ -188,15 +191,20 @@
 
     for k in range(HALF - 1):
         advance(k)
-    pl.semaphore_wait(barrier, nsec - 1 + 8)
+    pl.semaphore_wait(barrier, nsec - 1 + 4 + 7)
     offer(0)
-    for dz in (2, nz - 2):
-        signal(round_sem.at[0], chip_at(0, dz) * 2 + core, sec)
+    for dy in (2, 1, 3, 0):
+        if dy:
+            signal(round_sem.at[0], (base_y[dy] + my_z) * 2 + core, sec)
+        signal(round_sem.at[0], (base_y[dy] + my_z) * 2 + 1 - core, sec)
     for k in range(HALF - 1, STEPS - 1):
         advance(k)
     offer(1)
     advance(STEPS - 1)
     hpad[:, :, 0:8, :] = jnp.zeros((nsec, 4, 8, cells), F32)
+
+    for load in loads[5:]:
+        load.wait()
 
     own = jnp.broadcast_to(own_ref[...].astype(F32), (cells, cells))
     before = lax.broadcasted_iota(jnp.int32, (cells, cells), 0) < (
@@ -266,9 +274,8 @@
         packed = jnp.dot(pick[...], cur[c], preferred_element_type=F32)
         outs[c] = packed.astype(BF16).reshape(ntile, ROWS, seg)
 
-    def deliver(c):
-        def send(o, carry):
-            peer = tile_peer(o)
+    def deliver(c, offsets):
+        def send(peer):
             pltpu.make_async_remote_copy(
                 src_ref=outs.at[c, peer],
                 dst_ref=recv.at[c, tile],
@@ -277,23 +284,34 @@
                 device_id=(peer, sec),
                 device_id_type=MESH,
             ).start()
-            return carry
-
-        lax.fori_loop(0, ntile - 1, send, 0)
-        pltpu.make_async_copy(
-            outs.at[c, tile], recv.at[c, tile], recv_sem.at[1 + c]
-        ).start()
-
-    pl.semaphore_wait(round_sem.at[0], 2)
-    for dy in (2, 1, 3):
-        signal(round_sem.at[1], chip_at(dy, 0) * 2 + core, sec)
+
+        def send_all(base, at_own_z):
+            for other in (1, 0):
+                for dz in offsets:
+                    at = (base + at_z[dz]) * 2
+                    send(at + 1 - core if other else at + core)
+            if at_own_z:
+                send((base + my_z) * 2 + 1 - core)
+                if at_own_z == 2:
+                    send((base + my_z) * 2 + core)
+
+        along_y(lambda base: send_all(base, 2 if offsets is near else 0))
+        send_all(base_y[0], 1 if offsets is near else 0)
+        if offsets is near:
+            pltpu.make_async_copy(
+                outs.at[c, tile], recv.at[c, tile], recv_sem.at[1 + c]
+            ).start()
+
     currents(0)
-    pl.semaphore_wait(round_sem.at[1], 3)
-    signal(round_sem.at[2], chip * 2 + 1 - core, sec)
-    pl.semaphore_wait(round_sem.at[2], 1)
-    deliver(0)
+    pl.semaphore_wait(round_sem.at[0], 7)
+    for dz in (2, nz - 2):
+        signal(round_sem.at[1], (base_y[0] + at_z[dz]) * 2 + core, sec)
+    deliver(0, near)
     currents(1)
-    deliver(1)
+    pl.semaphore_wait(round_sem.at[1], 2)
+    deliver(0, far)
+    deliver(1, far)
+    deliver(1, near)
 
     count = jnp.broadcast_to(cnt_ref[...].astype(F32), (8, ntile)).astype(BF16)
     source = lax.broadcasted_iota(jnp.int32, (ntile, out_rows), 0)
@@ -352,11 +370,18 @@
         def read(n, carry, c=c):
             x = ordered[n]
             left_side = jnp.concatenate([x * mask for mask in masks], axis=1)
+            right_side = jnp.concatenate(
+                [
+                    w_ref[pl.ds(n * group, group), t].reshape(group * seg, -1)
+                    for t in range(2)
+                ],
+                axis=1,
+            )
+            both = jnp.dot(left_side, right_side, preferred_element_type=F32)
             for t in range(2):
-                right_side = w_ref[pl.ds(n * group, group), t].reshape(group * seg, -1)
-                tiles[c, t, pl.ds(pl.multiple_of(n * ROWS, ROWS), ROWS), :] = jnp.dot(
-                    left_side, right_side, preferred_element_type=F32
-                )
+                tiles[c, t, pl.ds(pl.multiple_of(n * ROWS, ROWS), ROWS), :] = both[
+                    :, t * seg : (t + 1) * seg
+                ]
             return carry
 
         lax.fori_loop(0, cells // group, read, 0, unroll=4)
@@ -373,28 +398,29 @@
                 preferred_element_type=F32,
             )
 
-    def give(o, carry):
-        peer = chip_peer(o)
+    partial[...] = part[...].astype(BF16).reshape(chips, STEPS, seg)
+
+    def give(peer_chip):
         pltpu.make_async_remote_copy(
-            src_ref=part.at[pl.ds(pl.multiple_of(peer * STEPS, STEPS), STEPS)],
+            src_ref=partial.at[peer_chip],
             dst_ref=first.at[chip],
             send_sem=send_sem.at[3],
             recv_sem=recv_sem.at[3],
-            device_id=(peer * 2 + core, sec),
+            device_id=(peer_chip * 2 + core, sec),
             device_id_type=MESH,
         ).start()
-        return carry
-
-    lax.fori_loop(0, chips - 1, give, 0)
-    pltpu.make_async_copy(
-        part.at[pl.ds(pl.multiple_of(chip * STEPS, STEPS), STEPS)],
-        first.at[chip],
-        recv_sem.at[3],
-    ).start()
+
+    def give_all(base):
+        for dz in far + near:
+            give(base + at_z[dz])
+
+    along_y(lambda base: (give_all(base), give(base + my_z)))
+    give_all(base_y[0])
+    pltpu.make_async_copy(partial.at[chip], first.at[chip], recv_sem.at[3]).start()
     pltpu.make_async_copy(first, first, recv_sem.at[3]).wait()
-    mine[...] = jnp.sum(first[...], axis=0)
-
-    for step in range(nsec):
+    mine[...] = jnp.sum(first[...].astype(F32), axis=0)
+
+    for step in (2, 1, 3, 0):
         for flip in range(2):
             if step or flip:
                 other_sec = lax.rem(sec + step, nsec)
@@ -424,17 +450,22 @@
     pltpu.make_async_copy(shared, shared, send_sem.at[4]).wait()
 
 
+def hand_over(fv_ref, probe_ref, fv_out, probe_out):
+    fv_out[...] = fv_ref[...]
+    probe_out[...] = probe_ref[...]
+
+
 def on_device(ny, nz, nsec, width, voltage, conductance, reversal, drive, inv_cable, owner_map, peer_counts, pattern, transfer):
     cells, seg = voltage.shape
     chips = ny * nz
     ntile = 2 * chips
     vmem = pl.BlockSpec(memory_space=pltpu.VMEM)
     rows = ntile * ROWS
-    return pl.pallas_call(
+    results = pl.pallas_call(
         functools.partial(kernel, ny, nz, nsec),
         out_shape=(
-            jax.ShapeDtypeStruct((cells, seg), F32),
-            jax.ShapeDtypeStruct((STEPS, width), F32),
+            pltpu.VMEM((cells, seg), F32),
+            pltpu.VMEM((STEPS, width), F32),
         ),
         in_specs=[pl.BlockSpec(memory_space=pl.ANY)] * 9,
         out_specs=(vmem, vmem),
@@ -463,12 +494,13 @@
             pltpu.VMEM((cells // 4, ROWS, seg), BF16),
             pltpu.VMEM((2, 2, cells * HALF, seg), F32),
             pltpu.VMEM((chips * STEPS, seg), F32),
-            pltpu.VMEM((chips, STEPS, seg), F32),
+            pltpu.VMEM((chips, STEPS, seg), BF16),
+            pltpu.VMEM((chips, STEPS, seg), BF16),
             pltpu.VMEM((STEPS, seg), F32),
             pltpu.VMEM((2 * nsec, STEPS, seg), F32),
             pltpu.SemaphoreType.DMA((8,)),
             pltpu.SemaphoreType.DMA,
-            pltpu.SemaphoreType.REGULAR((3,)),
+            pltpu.SemaphoreType.REGULAR((2,)),
             pltpu.SemaphoreType.DMA((7,)),
             pltpu.SemaphoreType.DMA((7,)),
         ],
@@ -487,6 +519,16 @@
         pattern[0].T,
         transfer,
     )
+    return pl.pallas_call(
+        hand_over,
+        out_shape=(
+            jax.ShapeDtypeStruct((cells, seg), F32),
+            jax.ShapeDtypeStruct((STEPS, width), F32),
+        ),
+        in_specs=[vmem, vmem],
+        out_specs=(vmem, vmem),
+        name="hand_over",
+    )(*(pltpu.with_memory_space_constraint(x, pltpu.VMEM) for x in results))
 
 
 def solution(mesh):

time: 46.3 us -> 41.9 us (0.905)
  local copies, waits for them, and re-layouts: 2.74 us -> 0 us
  Pallas kernels: 42.7 us -> 41.1 us
    unnamed x2 -> x0, local copies, waits for them, and re-layouts: 2.74 us -> none
    pallas_call x1 -> x2, Pallas kernels: 42.7 us -> 41.1 us  [the longest x1 40.5 us: on_device(): pl.pallas_call(functools.partial(kernel, ny, nz, nsec), out_shape=(pltpu....]
where the time goes in v3:
time: 41.9 us; the launch traced here: 41.8 us
  Pallas kernels  41.1 us (98%)
  between operations  0.64 us (2%)
    pallas_call x1, Pallas kernels, on_device(): pl.pallas_call(functools.partial(kernel, ny, nz, nsec), out_shape=(pltpu....  40.5 us

profile of v3, /device:TPU:1, one launch (start us, length us, event | category | flops | bytes accessed | tf_op | source)
XLA Modules:
  0.0 41.8 jit_solution(4139939768393956950)
XLA Ops:
  0.6 40.5 %cable_probe.1 = (f32[128,128]{1,0:T(8,128)S(1)}, f32[8,16]{1,0:T(8,128)S(1)}) custom-call(f32[128,128]{1,0:T(8,128)} %v_hbm.1, f32[128,128]{1,0:T(8,128)} %g_hbm.1, f32[128,128]{1,0:T(8,128)} %e_hbm.1, bf16[8,128,128]{2,1,0:T(8,128)(2,1)} %d_hbm.1, f32[128,128]{1,0:T(8,128)} %a_hbm.1, s32[1,128]{1,0:T(1,128)} %bitcast.5, s32[1,64]{1,0:T(1,128)} %cnt_hbm.1, ...), custom_call_target="tpu_custom_call" | custom-call | tf_op jit(solution)/shard_map/cable_probe/pallas_call | solution.py:464
  41.1 0.6 %hand_over.1 = (f32[128,128]{1,0:T(8,128)}, f32[8,16]{1,0:T(8,128)}) custom-call(f32[128,128]{1,0:T(8,128)S(1)} %get-tuple-element.4.fv_ref, f32[8,16]{1,0:T(8,128)S(1)} %get-tuple-element.5.probe_ref), custom_call_target="tpu_custom_call" | custom-call | tf_op jit(solution)/shard_map/hand_over/pallas_call | solution.py:522

commit v4 on v3

--- a/solution.py
+++ b/solution.py
@@ -57,6 +57,8 @@
     hl,
     hr,
     ends,
+    ends_out,
+    ends_in,
     got,
     hpad,
     zpad,
@@ -178,16 +180,19 @@
                 ends[c, pl.ds(2 * HALF * n + HALF + k, 1), :] = source[
                     at, pl.ds(seg - 1, 1), :
                 ]
-        for step in range(1, nsec):
+        ends_out[c] = ends[c].astype(BF16)
+        for step in (2, 1, 3):
             pltpu.make_async_remote_copy(
-                src_ref=ends.at[c],
-                dst_ref=got.at[c, sec],
+                src_ref=ends_out.at[c],
+                dst_ref=ends_in.at[c, sec],
                 send_sem=send_sem.at[5 + c],
                 recv_sem=recv_sem.at[5 + c],
                 device_id=(tile, lax.rem(sec + step, nsec)),
                 device_id_type=MESH,
             ).start()
-        pltpu.make_async_copy(ends.at[c], got.at[c, sec], recv_sem.at[5 + c]).start()
+        pltpu.make_async_copy(
+            ends_out.at[c], ends_in.at[c, sec], recv_sem.at[5 + c]
+        ).start()
 
     for k in range(HALF - 1):
         advance(k)
@@ -227,7 +232,8 @@
     lax.fori_loop(0, blocks, build_pick, 0)
 
     def meet(c):
-        pltpu.make_async_copy(got.at[c], got.at[c], recv_sem.at[5 + c]).wait()
+        pltpu.make_async_copy(ends_in.at[c], ends_in.at[c], recv_sem.at[5 + c]).wait()
+        got[c] = ends_in[c].astype(F32)
         known = (c + 1) * HALF
         for s in range(nsec):
             for q in range(2):
@@ -271,10 +277,16 @@
             cur[c, k_in * cells : (k_in + 1) * cells, :] = current
             if k == STEPS:
                 fv_ref[...] = now
-        packed = jnp.dot(pick[...], cur[c], preferred_element_type=F32)
-        outs[c] = packed.astype(BF16).reshape(ntile, ROWS, seg)
-
-    def deliver(c, offsets):
+
+    def pack(c, base):
+        size = 2 * nz * ROWS
+        rows = pl.ds(pl.multiple_of(base * (2 * ROWS), size), size)
+        packed = jnp.dot(pick[rows, :], cur[c], preferred_element_type=F32)
+        outs[c, pl.ds(base * 2, 2 * nz)] = packed.astype(BF16).reshape(
+            2 * nz, ROWS, seg
+        )
+
+    def deliver(c, offsets, fresh):
         def send(peer):
             pltpu.make_async_remote_copy(
                 src_ref=outs.at[c, peer],
@@ -286,6 +298,8 @@
             ).start()
 
         def send_all(base, at_own_z):
+            if fresh:
+                pack(c, base)
             for other in (1, 0):
                 for dz in offsets:
                     at = (base + at_z[dz]) * 2
@@ -306,12 +320,12 @@
     pl.semaphore_wait(round_sem.at[0], 7)
     for dz in (2, nz - 2):
         signal(round_sem.at[1], (base_y[0] + at_z[dz]) * 2 + core, sec)
-    deliver(0, near)
+    deliver(0, near, True)
     currents(1)
     pl.semaphore_wait(round_sem.at[1], 2)
-    deliver(0, far)
-    deliver(1, far)
-    deliver(1, near)
+    deliver(0, far, False)
+    deliver(1, far, True)
+    deliver(1, near, False)
 
     count = jnp.broadcast_to(cnt_ref[...].astype(F32), (8, ntile)).astype(BF16)
     source = lax.broadcasted_iota(jnp.int32, (ntile, out_rows), 0)
@@ -384,7 +398,7 @@
                 ]
             return carry
 
-        lax.fori_loop(0, cells // group, read, 0, unroll=4)
+        lax.fori_loop(0, cells // group, read, 0, unroll=8)
 
         for k_in in range(HALF):
             sums = jnp.concatenate(
@@ -440,7 +454,7 @@
     probe_ref[...] = pltpu.roll(summed, lax.rem(seg - line * width, seg), 1)[:, :width]
 
     for c in range(2):
-        told = got.at[c, pl.ds(0, nsec - 1)]
+        told = ends_in.at[c, pl.ds(0, nsec - 1)]
         pltpu.make_async_copy(told, told, send_sem.at[5 + c]).wait()
         sent = outs.at[c, pl.ds(0, ntile - 1)]
         pltpu.make_async_copy(sent, sent, send_sem.at[1 + c]).wait()
@@ -483,6 +497,8 @@
             pltpu.VMEM((LAGS, seg, cells), F32),
             pltpu.VMEM((LAGS, seg, cells), F32),
             pltpu.VMEM((2, 6 * HALF, cells), F32),
+            pltpu.VMEM((2, 6 * HALF, cells), BF16),
+            pltpu.VMEM((2, nsec, 6 * HALF, cells), BF16),
             pltpu.VMEM((2, nsec, 6 * HALF, cells), F32),
             pltpu.VMEM((nsec, 4, 16, cells), F32),
             pltpu.VMEM((nsec, 2, 8, cells), F32),

time: 41.9 us -> 40.5 us (0.967)
  Pallas kernels: 41.1 us -> 39.8 us
    pallas_call x1, Pallas kernels: 40.5 us -> 39.1 us  [on_device(): pl.pallas_call(functools.partial(kernel, ny, nz, nsec), out_shape=(pltpu....]
where the time goes in v4:
time: 40.5 us; the launch traced here: 40.4 us
  Pallas kernels  39.8 us (98%)
  between operations  0.64 us (2%)
    pallas_call x1, Pallas kernels, on_device(): pl.pallas_call(functools.partial(kernel, ny, nz, nsec), out_shape=(pltpu....  39.1 us

profile of v4, /device:TPU:1, one launch (start us, length us, event | category | flops | bytes accessed | tf_op | source)
XLA Modules:
  0.0 40.4 jit_solution(9561979661571583390)
XLA Ops:
  0.6 39.1 %cable_probe.1 = (f32[128,128]{1,0:T(8,128)S(1)}, f32[8,16]{1,0:T(8,128)S(1)}) custom-call(f32[128,128]{1,0:T(8,128)} %v_hbm.1, f32[128,128]{1,0:T(8,128)} %g_hbm.1, f32[128,128]{1,0:T(8,128)} %e_hbm.1, bf16[8,128,128]{2,1,0:T(8,128)(2,1)} %d_hbm.1, f32[128,128]{1,0:T(8,128)} %a_hbm.1, s32[1,128]{1,0:T(1,128)} %bitcast.5, s32[1,64]{1,0:T(1,128)} %cnt_hbm.1, ...), custom_call_target="tpu_custom_call" | custom-call | tf_op jit(solution)/shard_map/cable_probe/pallas_call | solution.py:478
  39.8 0.6 %hand_over.1 = (f32[128,128]{1,0:T(8,128)}, f32[8,16]{1,0:T(8,128)}) custom-call(f32[128,128]{1,0:T(8,128)S(1)} %get-tuple-element.4.fv_ref, f32[8,16]{1,0:T(8,128)S(1)} %get-tuple-element.5.probe_ref), custom_call_target="tpu_custom_call" | custom-call | tf_op jit(solution)/shard_map/hand_over/pallas_call | solution.py:538

commit v5 on v4

--- a/solution.py
+++ b/solution.py
@@ -321,9 +321,9 @@
     for dz in (2, nz - 2):
         signal(round_sem.at[1], (base_y[0] + at_z[dz]) * 2 + core, sec)
     deliver(0, near, True)
-    currents(1)
     pl.semaphore_wait(round_sem.at[1], 2)
     deliver(0, far, False)
+    currents(1)
     deliver(1, far, True)
     deliver(1, near, False)
 
@@ -398,7 +398,7 @@
                 ]
             return carry
 
-        lax.fori_loop(0, cells // group, read, 0, unroll=8)
+        lax.fori_loop(0, cells // group, read, 0, unroll=16)
 
         for k_in in range(HALF):
             sums = jnp.concatenate(

time: 40.5 us -> 40.3 us (level)
  no operation moved by 1% of the time
where the time goes in v5:
time: 40.3 us; the launch traced here: 40.2 us
  Pallas kernels  39.6 us (98%)
  between operations  0.64 us (2%)
    pallas_call x1, Pallas kernels, on_device(): pl.pallas_call(functools.partial(kernel, ny, nz, nsec), out_shape=(pltpu....  38.9 us

profile of v5, /device:TPU:1, one launch (start us, length us, event | category | flops | bytes accessed | tf_op | source)
XLA Modules:
  0.0 40.2 jit_solution(17039983033389028947)
XLA Ops:
  0.6 38.9 %cable_probe.1 = (f32[128,128]{1,0:T(8,128)S(1)}, f32[8,16]{1,0:T(8,128)S(1)}) custom-call(f32[128,128]{1,0:T(8,128)} %v_hbm.1, f32[128,128]{1,0:T(8,128)} %g_hbm.1, f32[128,128]{1,0:T(8,128)} %e_hbm.1, bf16[8,128,128]{2,1,0:T(8,128)(2,1)} %d_hbm.1, f32[128,128]{1,0:T(8,128)} %a_hbm.1, s32[1,128]{1,0:T(1,128)} %bitcast.5, s32[1,64]{1,0:T(1,128)} %cnt_hbm.1, ...), custom_call_target="tpu_custom_call" | custom-call | tf_op jit(solution)/shard_map/cable_probe/pallas_call | solution.py:478
  39.6 0.6 %hand_over.1 = (f32[128,128]{1,0:T(8,128)}, f32[8,16]{1,0:T(8,128)}) custom-call(f32[128,128]{1,0:T(8,128)S(1)} %get-tuple-element.4.fv_ref, f32[8,16]{1,0:T(8,128)S(1)} %get-tuple-element.5.probe_ref), custom_call_target="tpu_custom_call" | custom-call | tf_op jit(solution)/shard_map/hand_over/pallas_call | solution.py:538

commit v6 on v5

--- a/solution.py
+++ b/solution.py
@@ -135,10 +135,8 @@
             signal(barrier, (base_y[dy] + my_z) * 2 + core, sec)
         signal(barrier, (base_y[dy] + my_z) * 2 + 1 - core, sec)
 
-    for load in loads[:5]:
+    for load in loads[:4]:
         load.wait()
-    w_copy = pltpu.make_async_copy(w_hbm.at[0], w_ref, w_sem)
-    w_copy.start()
 
     a = a_ref[...]
     a_high, a_low = split(a)
@@ -194,6 +192,9 @@
             ends_out.at[c], ends_in.at[c, sec], recv_sem.at[5 + c]
         ).start()
 
+    loads[4].wait()
+    w_copy = pltpu.make_async_copy(w_hbm.at[0], w_ref, w_sem)
+    w_copy.start()
     for k in range(HALF - 1):
         advance(k)
     pl.semaphore_wait(barrier, nsec - 1 + 4 + 7)

time: 40.3 us -> 40.3 us (level)
  no operation moved by 1% of the time
where the time goes in v6:
time: 40.3 us; the launch traced here: 40.2 us
  Pallas kernels  39.6 us (98%)
  between operations  0.64 us (2%)
    pallas_call x1, Pallas kernels, on_device(): pl.pallas_call(functools.partial(kernel, ny, nz, nsec), out_shape=(pltpu....  38.9 us

profile of v6, /device:TPU:1, one launch (start us, length us, event | category | flops | bytes accessed | tf_op | source)
XLA Modules:
  0.0 40.2 jit_solution(1699614598688770506)
XLA Ops:
  0.6 38.9 %cable_probe.1 = (f32[128,128]{1,0:T(8,128)S(1)}, f32[8,16]{1,0:T(8,128)S(1)}) custom-call(f32[128,128]{1,0:T(8,128)} %v_hbm.1, f32[128,128]{1,0:T(8,128)} %g_hbm.1, f32[128,128]{1,0:T(8,128)} %e_hbm.1, bf16[8,128,128]{2,1,0:T(8,128)(2,1)} %d_hbm.1, f32[128,128]{1,0:T(8,128)} %a_hbm.1, s32[1,128]{1,0:T(1,128)} %bitcast.5, s32[1,64]{1,0:T(1,128)} %cnt_hbm.1, ...), custom_call_target="tpu_custom_call" | custom-call | tf_op jit(solution)/shard_map/cable_probe/pallas_call | solution.py:479
  39.6 0.6 %hand_over.1 = (f32[128,128]{1,0:T(8,128)}, f32[8,16]{1,0:T(8,128)}) custom-call(f32[128,128]{1,0:T(8,128)S(1)} %get-tuple-element.4.fv_ref, f32[8,16]{1,0:T(8,128)S(1)} %get-tuple-element.5.probe_ref), custom_call_target="tpu_custom_call" | custom-call | tf_op jit(solution)/shard_map/hand_over/pallas_call | solution.py:539
